TPU v7x, 32 devices: a whole 2x2x4 slice. The times are simulated.
32 devices in a mesh: group: 2 (over x), lon: 8 (over z, y), lat: 2 (over core).
Axes of the slice: x: 2, y: 2, z: 4, core: 2. Of those that a mesh axis runs over, the one named last changes fastest.
Arguments:
- tokens: bfloat16 [128, 256, 384], P(('group', 'lat'), 'lon'), parts along dimension 0, may hold values from -6 to 6
- visible: int32 [128, 256], P(('group', 'lat'), 'lon'), parts along dimension 0, may hold values 0 or 1
- mask_token: bfloat16 [384], replicated, may hold values from -4 to 4
- norm_gain_table: float32 [2, 384], replicated, may hold values from 0.25 to 1.75
- query_key_value_weight: bfloat16 [2, 384, 1152], replicated, may hold values from -0.3125 to 0.3125
- output_weight: bfloat16 [2, 384, 384], replicated, may hold values from -0.3125 to 0.3125
- cotangent: float32 [128, 256, 384], P(('group', 'lat'), 'lon'), parts along dimension 0, may hold values from -6 to 6
Outputs:
- grad_tokens: float32 [128, 256, 384], P(('group', 'lat'), 'lon'), parts along dimension 0
- grad_qkv: float32 [4, 384, 1152], P('group'), parts along dimension 0
- grad_out: float32 [4, 384, 384], P('group'), parts along dimension 0
- grad_gain: float32 [4, 384], P('group'), parts along dimension 0
There are 2 independent parts, one for each index of `group`. A program takes and returns all parts, laid end to end along the dimension named above; an argument that names none is the same for every part. Nothing has to cross between parts.
Inputs may be any that keep to these rules, and one draw needn't show every extreme that they name: 1 marks a visible token.
All inputs are finite; a program needn't handle non-finite values. No bound on the sum of `visible` on one device may be relied on, other than what follows from the above.
Results may differ from a plain program's by a relative error of at most 0.01.
Values may be sent and summed in bfloat16 or wider, within the bound.
No kernel may reach another device: no remote copies, remote signals or barrier semaphores. Data moves between devices by JAX's collectives and lax.ppermute only.
A program may use at most 320 MiB of HBM per device.

v0:
```python
import functools

import jax
import jax.numpy as jnp
import numpy as np
from jax import lax
from jax.experimental import pallas as pl
from jax.experimental.pallas import tpu as pltpu
from jax.sharding import PartitionSpec as P

HEADS = 6
EPS = 1e-05
F32 = jnp.float32
BF16 = jnp.bfloat16
LARGE_MIB = 56
HALO = 112
CORNER = 96
KEYS = 208
RETURNED = 224


def nn(a, b):
    return lax.dot_general(a, b, (((1,), (0,)), ((), ())), preferred_element_type=F32)


def nt(a, b):
    return lax.dot_general(a, b, (((1,), (1,)), ((), ())), preferred_element_type=F32)


def tn(a, b):
    return lax.dot_general(a, b, (((0,), (0,)), ((), ())), preferred_element_type=F32)


def tt(a, b):
    return lax.dot_general(a, b, (((0,), (1,)), ((), ())), preferred_element_type=F32)


def iota(shape, dim):
    return lax.broadcasted_iota(jnp.int32, shape, dim)


def one_hot(condition):
    return jnp.where(condition, 1.0, 0.0).astype(BF16)


def permuted(value, axis, target):
    count = lax.axis_size(axis)
    return lax.ppermute(value, axis, [(i, target(i) % count) for i in range(count)])


def lat_swap(value):
    return permuted(value, "lat", lambda i: i ^ 1)


def lon_swap(value):
    return permuted(value, "lon", lambda i: i ^ 1)


def lon_forward(value):
    return permuted(value, "lon", lambda i: i + 2 if i % 2 == 0 else i - 2)


def lon_backward(value):
    return permuted(value, "lon", lambda i: i - 2 if i % 2 == 0 else i + 2)


def from_left(value):
    return permuted(value, "lon", lambda i: i + 1)


def from_right(value):
    return permuted(value, "lon", lambda i: i - 1)


def chained(value, after):
    return lax.optimization_barrier((value, after))


def exchanged(parts, axis_stride, factor):
    count = lax.axis_size("lon")
    digit = (lax.axis_index("lon") // axis_stride) % factor
    moved = []
    for d in range(1, factor):
        pairs = [(i, shifted(i, axis_stride, factor, d)) for i in range(count)]
        moved.append(lax.ppermute(parts(digit ^ d), "lon", pairs))
    total = parts(digit).astype(F32)
    for piece in moved:
        total = total + piece.astype(F32)
    return total.astype(BF16)


def shifted(i, stride, factor, d):
    digit = (i // stride) % factor
    return i + ((digit ^ d) - digit) * stride


def spread(value, axis_stride, factor):
    count = lax.axis_size("lon")
    digit = (lax.axis_index("lon") // axis_stride) % factor
    rows = value.shape[0]
    full = jnp.zeros((factor * rows,) + value.shape[1:], value.dtype)
    full = lax.dynamic_update_slice(full, value, (digit * rows, 0))
    for d in range(1, factor):
        pairs = [(i, shifted(i, axis_stride, factor, d)) for i in range(count)]
        got = lax.ppermute(value, "lon", pairs)
        at = (digit ^ d) * rows
        full = lax.dynamic_update_slice(full, got, (at, 0))
    return full


def lon_factors():
    left = lax.axis_size("lon")
    stride, out = 1, []
    for factor in [2] + [4] * 10:
        if left == 1:
            break
        factor = min(factor, left)
        out.append((stride, factor))
        stride, left = stride * factor, left // factor
    return out


def halves_summed(mine, other):
    return (mine.astype(F32) + lat_swap(other).astype(F32)).astype(BF16)


def stage_summed(value, stage):
    stride, factor = stage
    size = value.shape[0] // factor
    return exchanged(
        lambda k: lax.dynamic_slice_in_dim(value, k * size, size, 0), stride, factor
    )


def norm_parts(x):
    mean = jnp.mean(x, axis=-1, keepdims=True)
    centred = x - mean
    spread = jnp.mean(centred * centred, axis=-1, keepdims=True)
    rstd = lax.rsqrt(spread + EPS)
    return centred * rstd, rstd


def norm_back(x, gain, grad_normal):
    xhat, rstd = norm_parts(x)
    g = grad_normal * gain
    return rstd * (
        g - jnp.mean(g, axis=-1, keepdims=True) - xhat * jnp.mean(g * xhat, axis=-1, keepdims=True)
    )


def shown_column(visible, token):
    rows, cols = visible.shape
    tile = token.shape[0]
    of_row = nn(one_hot(token // cols == iota((tile, rows), 1)), visible.astype(F32).astype(BF16))
    mine = token % cols == iota((tile, cols), 1)
    return jnp.sum(jnp.where(mine, of_row, 0.0), axis=1, keepdims=True)


def token_order(rows, cols):
    row, col = np.divmod(np.arange(rows * cols), cols)
    border = (row == 0) | (row == rows - 1) | (col == 0) | (col == cols - 1)
    order = np.argsort(~border, kind="stable").astype(np.int32)
    return order, np.argsort(order, kind="stable").astype(np.int32)


def picked(places, values):
    count = values.shape[0]
    return nn(one_hot(places == iota((places.shape[0], count), 1)), values)


def start_kernel(order_ref, tok_ref, vis_ref, mask_ref, gain_ref, start_ref, normal_ref):
    width = tok_ref.shape[1]
    token = order_ref[...]
    shown = shown_column(vis_ref[...], token)
    x = jnp.where(
        shown > 0.5, picked(token, tok_ref[...]), mask_ref[...].astype(F32).reshape(1, width)
    )
    start_ref[...] = x.astype(BF16)
    xhat, _ = norm_parts(x)
    normal_ref[...] = (xhat * gain_ref[0:1, :]).astype(BF16)


def first_kernel(
    lat_ref, order_ref, n0, n1, n2, n3, n4, n5, start_ref,
    wt_ref, wo_ref, gain_ref,
    q_ref, kv_ref, p_ref, mixed_ref, h_ref, normal_ref, row_ref, left_ref, right_ref,
    w_s, pack_s,
):
    width, tile = q_ref.shape
    head = width // HEADS
    blocks = (n0, n1, n2, n3, n4, n5)
    q_ref[...] = nt(wt_ref[0:width], n0[...]).astype(BF16)
    for b, ref in enumerate(blocks):
        kv_ref[b] = nt(wt_ref[width : 3 * width], ref[...]).astype(BF16)
    for h in range(HEADS):
        lo, hi = h * head, (h + 1) * head
        q = q_ref[lo:hi, :].astype(F32) * (head**-0.5)
        total = jnp.zeros((1, tile), F32)
        out = jnp.zeros((head, tile), F32)
        for b in range(len(blocks)):
            k = kv_ref[b, lo:hi, :].astype(F32)
            w = jnp.exp(jnp.sum(q * k, axis=0, keepdims=True))
            w_s[b, h : h + 1, :] = w
            total = total + w
            out = out + w * kv_ref[b, width + lo : width + hi, :].astype(F32)
        inverse = 1.0 / total
        for b in range(len(blocks)):
            p_ref[b, h : h + 1, :] = w_s[b, h : h + 1, :] * inverse
        mixed_ref[lo:hi, :] = (out * inverse).astype(BF16)
    h1 = start_ref[...].astype(F32) + tn(mixed_ref[...], wo_ref[...])
    h1 = h1.astype(BF16)
    h_ref[...] = h1
    xhat, _ = norm_parts(h1.astype(F32))
    normal = (xhat * gain_ref[1:2, :]).astype(BF16)
    normal_ref[...] = normal
    step = pl.program_id(0)
    brow = jnp.where(lat_ref[0] == 0, 31, 0)
    slot = iota((96, tile), 0)
    r, c = order_ref[...] // 32, order_ref[...] % 32
    pick = one_hot(
        ((slot < 32) & (r == brow) & (c == slot))
        | ((slot >= 32) & (slot < 64) & (c == 0) & (r == slot - 32))
        | ((slot >= 64) & (c == 31) & (r == slot - 64))
    )

    @pl.when(step == 0)
    def _():
        pack_s[...] = jnp.zeros_like(pack_s)

    pack_s[...] += nn(pick, normal)

    @pl.when(step == pl.num_programs(0) - 1)
    def _():
        for i, ref in enumerate((row_ref, left_ref, right_ref)):
            ref[...] = pack_s[i * 32 : i * 32 + 32, :].astype(BF16)


def write_halves(lat, total_ref, mine_ref, other_ref):
    half = mine_ref.shape[0]
    for band in range(2):

        @pl.when(lat == band)
        def _():
            mine_ref[...] = total_ref[band * half : (band + 1) * half, :].astype(BF16)
            other_ref[...] = total_ref[(1 - band) * half : (2 - band) * half, :].astype(BF16)


def second_kernel(
    lat_ref, place_ref, na_ref, nb_ref, row_ref, left_ref, right_ref, dleft_ref, dright_ref,
    w_all, wo_all, cot_ref,
    both_ref, dw_ref, brow_ref, bleft_ref, bright_ref,
    dq_ref, dk_ref, dv_ref, mixed_s, dkh_ref, dvh_ref, halo_s,
    q_s, k_s, v_s, kc_s, vc_s, dk_s, dv_s, dkc_s, dvc_s, do_s, mask_s, normal_s,
):
    points, width = cot_ref.shape
    head = width // HEADS
    w_ref, wo_ref = w_all.at[1], wo_all.at[1]
    upper = lat_ref[0] == 0
    halo_s[0:32, :] = row_ref[...]
    halo_s[32:64, :] = left_ref[...]
    halo_s[64:96, :] = right_ref[...]
    a, b = iota((16, 32), 0), iota((16, 32), 1)
    sent = b == jnp.where(upper, 0, 31)
    corners = nn(one_hot(sent & (a == 0)), dleft_ref[...])
    corners += nn(one_hot(sent & (a == 1)), dright_ref[...])
    halo_s[CORNER:HALO, :] = corners.astype(BF16)
    halo = halo_s[...]
    ordered = jnp.concatenate([na_ref[...], nb_ref[...]], 0)
    @pl.loop(0, points // 256)
    def _(step):
        rows = pl.ds(pl.multiple_of(step * 256, 256), 256)
        normal_s[rows, :] = picked(place_ref[rows, :], ordered).astype(BF16)
    normal = normal_s[...]
    scale = head**-0.5
    q_s[...] = (nn(normal, w_ref[:, 0:width]).astype(BF16).astype(F32) * scale).astype(BF16)
    k_s[32 : 32 + points, :] = nn(normal, w_ref[:, width : 2 * width]).astype(BF16)
    v_s[32 : 32 + points, :] = nn(normal, w_ref[:, 2 * width : 3 * width]).astype(BF16)
    kh = nn(halo, w_ref[:, width : 2 * width]).astype(BF16)
    vh = nn(halo, w_ref[:, 2 * width : 3 * width]).astype(BF16)
    for at in (0, 32 + points):
        k_s[at : at + 32, :] = kh[0:32]
        v_s[at : at + 32, :] = vh[0:32]
    tiles = points // 128
    slots = tiles * 16
    a, b = iota((slots, HALO - 32), 0), iota((slots, HALO - 32), 1)
    place, is_right = a % 16, jnp.where(a % 16 >= 6, 1, 0)
    ext_row = 4 * (a // 16) + place - 6 * is_right
    inner = (ext_row >= 1) & (ext_row <= 32)
    source = jnp.where(inner, 32 * is_right + ext_row - 1, 64 + is_right)
    spread_cols = one_hot((place < 12) & (b == source))
    kc_s[...] = nn(spread_cols, kh[32:HALO]).astype(BF16)
    vc_s[...] = nn(spread_cols, vh[32:HALO]).astype(BF16)
    dk_s[...] = jnp.zeros_like(dk_s)
    dv_s[...] = jnp.zeros_like(dv_s)
    cot = cot_ref[...].astype(BF16)
    both_ref[:, width : 2 * width] = cot
    do_s[...] = nt(cot, wo_ref[...]).astype(BF16)

    key, query = iota((KEYS, 256), 0), iota((KEYS, 256), 1) % 128
    place = key - 192
    right = place >= 6
    row = jnp.where(place < 0, key // 32, jnp.where(right, place - 6, place))
    col = jnp.where(place < 0, key % 32, jnp.where(right, 32, -1))
    near = (jnp.abs(row - 1 - query // 32) <= 1) & (jnp.abs(col - query % 32) <= 1)
    mask_s[...] = jnp.where(near & (place < 12), row, 9)

    def tile_step(t, carry):
        base = pl.multiple_of(t * 128, 128)
        first = jnp.where(upper & (t == 0), 1, 0)
        last = jnp.where(jnp.logical_not(upper) & (t == tiles - 1), 4, 5)
        mask = (mask_s[...] >= first) & (mask_s[...] <= last)
        even = iota((128, 128), 1) < 64
        top = iota((128, 128), 0) < 64
        win, here = pl.ds(base, 192), pl.ds(base, 128)
        side = pl.ds(pl.multiple_of(t * 16, 16), 16)
        for pair in range(HEADS // 2):
            lanes = slice(pair * 128, pair * 128 + 128)
            q = q_s[here, lanes]
            do = do_s[here, lanes]
            zero = jnp.zeros_like(q)
            qm = jnp.concatenate([jnp.where(even, q, zero), jnp.where(even, zero, q)], 0)
            dom = jnp.concatenate([jnp.where(even, do, zero), jnp.where(even, zero, do)], 0)
            k = jnp.concatenate([k_s[win, lanes], kc_s[side, lanes]], 0)
            v = jnp.concatenate([v_s[win, lanes], vc_s[side, lanes]], 0)
            w = jnp.where(mask, jnp.exp(nt(k, qm)), 0.0)
            p = w * (1.0 / jnp.sum(w, axis=0, keepdims=True))
            dp = nt(v, dom)
            delta = jnp.sum(p * dp, axis=0, keepdims=True)
            ds = (p * (dp - delta)).astype(BF16)
            p = p.astype(BF16)
            out = tn(v, p)
            mixed_s[lanes, here] = jnp.where(top, out[:, 0:128], out[:, 128:256]).astype(BF16)
            dq = tn(k, ds) * scale
            dq_ref[lanes, here] = jnp.where(top, dq[:, 0:128], dq[:, 128:256]).astype(BF16)
            dk, dv = nn(ds, qm), nn(p, dom)
            dk_s[win, lanes] += dk[0:192]
            dv_s[win, lanes] += dv[0:192]
            dkc_s[side, lanes] = dk[192:KEYS].astype(BF16)
            dvc_s[side, lanes] = dv[192:KEYS].astype(BF16)
        return carry

    lax.fori_loop(0, tiles, tile_step, 0)

    row_at = pl.multiple_of(jnp.where(upper, 32 + points, 0), 32)
    dkh = jnp.concatenate([dk_s[pl.ds(row_at, 32), :], tn(spread_cols, dkc_s[...])], 0).astype(BF16)
    dvh = jnp.concatenate([dv_s[pl.ds(row_at, 32), :], tn(spread_cols, dvc_s[...])], 0).astype(BF16)
    dkh_ref[...] = dkh
    dvh_ref[...] = dvh
    dk_ref[...] = dk_s[32 : 32 + points, :].astype(BF16)
    dv_ref[...] = dv_s[32 : 32 + points, :].astype(BF16)
    wk, wv = (w_ref[:, i * width : (i + 1) * width] for i in (1, 2))
    back = (nt(dkh, wk) + nt(dvh, wv)).astype(BF16)
    brow_ref[...] = back[0:32]
    for ref, at in ((bleft_ref, 32), (bright_ref, 64)):
        ref[0:32, :] = back[at : at + 32]
        ref[32:48, :] = back[CORNER:HALO]
    wq, wk, wv = (w_all[1, :, i * width : (i + 1) * width] for i in range(3))
    dw_ref[0:width, :] = nn(dq_ref[...], normal).astype(BF16)
    dw_ref[width : 2 * width, :] = (tn(dk_ref[...], normal) + tn(dkh_ref[...], halo)).astype(BF16)
    dw_ref[2 * width : 3 * width, :] = (
        tn(dv_ref[...], normal) + tn(dvh_ref[...], halo)
    ).astype(BF16)
    dw_ref[3 * width : 4 * width, :] = nn(mixed_s[...], cot).astype(BF16)
    both_ref[:, 0:width] = (tt(dq_ref[...], wq) + nt(dk_ref[...], wk) + nt(dv_ref[...], wv)).astype(BF16)


def third_kernel(
    lat_ref, order_ref, n0, n1, n2, n3, n4, n5, q_ref, kv_ref, p_ref, mixed_ref, h_ref, both_ref,
    packs_ref, wt_ref, wo_ref, gain_ref, dw_in,
    dh_ref, d0, d1, d2, d3, d4, d5, dw_ref, other_ref,
    dw_s, dmix_s, dkv_s, dq_s, dp_s, n_s,
):
    width, tile = q_ref.shape
    head = width // HEADS
    scale = head**-0.5
    blocks = (n0, n1, n2, n3, n4, n5)
    outs = (d0, d1, d2, d3, d4, d5)
    step = pl.program_id(0)

    @pl.when(step == 0)
    def _():
        dw_s[...] = jnp.zeros_like(dw_s) if dw_in is None else dw_in[...]

    token = order_ref[...]
    both = picked(token, both_ref[...])
    dn = both[:, 0:width]
    if packs_ref is not None:
        brow = jnp.where(lat_ref[0] == 0, 31, 0)
        r, c, slot = token // 32, token % 32, iota((tile, RETURNED), 1)
        border = r == brow
        place = one_hot(
            (border & (slot < 32) & (slot == c))
            | ((c == 0) & (slot < 64) & (slot == 32 + r))
            | ((c == 31) & (slot < 112) & (slot == 80 + r))
            | (border & (c == 0) & (slot == 128 + 33))
            | (border & (c == 31) & (slot == 176 + 32))
        )
        dn = dn + nn(place, packs_ref[...])
    dh = norm_back(h_ref[...].astype(F32), gain_ref[1:2, :], dn)
    dh_ref[...] = dh
    dh = dh + both[:, width : 2 * width]
    dhb = dh.astype(BF16)
    dmix_s[...] = nt(wo_ref[...], dhb)
    dw_s[3 * width : 4 * width, :] += nn(mixed_ref[...], dhb)
    for h in range(HEADS):
        lo, hi = h * head, (h + 1) * head
        dmix = dmix_s[lo:hi, :]
        delta = jnp.zeros((1, tile), F32)
        for b in range(len(blocks)):
            dp = jnp.sum(
                dmix * kv_ref[b, width + lo : width + hi, :].astype(F32), axis=0, keepdims=True
            )
            dp_s[b : b + 1, :] = dp
            delta = delta + p_ref[b, h : h + 1, :] * dp
        q = q_ref[lo:hi, :].astype(F32)
        dq = jnp.zeros((head, tile), F32)
        for b in range(len(blocks)):
            p = p_ref[b, h : h + 1, :]
            ds = p * (dp_s[b : b + 1, :] - delta) * scale
            dq = dq + ds * kv_ref[b, lo:hi, :].astype(F32)
            here = slice(b * tile, (b + 1) * tile)
            dkv_s[lo:hi, here] = (ds * q).astype(BF16)
            dkv_s[width + lo : width + hi, here] = (p * dmix).astype(BF16)
        dq_s[lo:hi, :] = dq.astype(BF16)
    dq = dq_s[...]
    dw_s[0:width, :] += nn(dq, n0[...])
    for b, ref in enumerate(blocks):
        n_s[b * tile : (b + 1) * tile, :] = ref[...]
    dw_s[width : 3 * width, :] += nn(dkv_s[...], n_s[...])
    grads = tn(dkv_s[...], wt_ref[width : 3 * width])
    outs[0][...] = grads[0:tile] + tn(dq, wt_ref[0:width])
    for b in range(1, len(blocks)):
        outs[b][...] = grads[b * tile : (b + 1) * tile].astype(BF16)

    @pl.when(step == pl.num_programs(0) - 1)
    def _():
        if other_ref is None:
            dw_ref[...] = dw_s[...]
        else:
            write_halves(lat_ref[0], dw_s, dw_ref, other_ref)


def last_kernel(place_ref, vis_ref, gain_ref, cot_ref, *refs):
    inputs, out_ref, high_s, low_s = refs[:-3], refs[-3], refs[-2], refs[-1]
    points, width = cot_ref.shape
    tile = 256
    at = 0
    while inputs:
        start_ref, dh_ref, own_ref, far_ref, near_ref = inputs[:5]
        for lo in range(0, start_ref.shape[0], tile):
            rows = slice(lo, lo + tile)
            dn = own_ref[rows] + far_ref[rows].astype(F32) + near_ref[rows].astype(F32)
            back = norm_back(start_ref[rows].astype(F32), gain_ref[0:1, :], dn)
            grad = dh_ref[rows] + back
            high = grad.astype(BF16)
            high_s[at : at + tile, :] = high
            low_s[at : at + tile, :] = (grad - high.astype(F32)).astype(BF16)
            at += tile
        inputs = inputs[5:]
    for lo in range(0, points, tile):
        rows = slice(lo, lo + tile)
        place = place_ref[rows, :]
        shown = shown_column(vis_ref[...], lo + iota((tile, 1), 0))
        grad = picked(place, high_s[...]) + picked(place, low_s[...]) + cot_ref[rows]
        out_ref[rows] = jnp.where(shown > 0.5, grad, 0.0)


def weights_kernel(
    factor, pieces, lat_ref, mine_ref, other_ref, wt_ref, gain_ref,
    qkv_ref, out_ref, gain_out_ref, rows_s,
):
    total, width = mine_ref.shape
    piece = total // pieces // 2
    lat = lat_ref[0]
    for ref, band in ((mine_ref, lat), (other_ref, 1 - lat)):
        for k in range(pieces):
            at = pl.multiple_of(band * (total // 2) + k * piece, 8)
            for layer in range(2):
                lo = (2 * k + layer) * piece
                rows_s[layer, pl.ds(at, piece), :] = ref[lo : lo + piece, :].astype(F32) * factor
    for layer in range(2):
        acc = jnp.zeros((1, width), F32)
        for i in range(3):
            lo, hi = i * width, (i + 1) * width
            grad = rows_s[layer, lo:hi, :]
            weight = wt_ref[layer, lo:hi, :].astype(F32)
            acc = acc + jnp.sum(weight * grad, axis=0, keepdims=True)
            qkv_ref[layer, :, lo:hi] = grad.T
        out_ref[layer] = rows_s[layer, 3 * width : 4 * width, :]
        gain_out_ref[layer : layer + 1, :] = acc / gain_ref[layer : layer + 1, :]


def call(
    kernel, out_shape, scratch=(), grid=None, in_specs=None, out_specs=None, us=1, aliases=None, mib=12
):
    return pl.pallas_call(
        kernel,
        out_shape=out_shape,
        grid_spec=pltpu.PrefetchScalarGridSpec(
            num_scalar_prefetch=0,
            grid=grid or (),
            in_specs=in_specs,
            out_specs=out_specs,
            scratch_shapes=list(scratch),
        ),
        input_output_aliases=aliases or {},
        cost_estimate=pl.CostEstimate(
            flops=int(us * 1e6 * 800), bytes_accessed=int(us * 1e6), transcendentals=0
        ),
        compiler_params=pltpu.CompilerParams(vmem_limit_bytes=mib * 1024 * 1024),
    )


def whole():
    return pl.BlockSpec(memory_space=pltpu.VMEM)


def scalar():
    return pl.BlockSpec(memory_space=pltpu.SMEM)


def fixed(shape):
    return pl.BlockSpec(shape, lambda i: (0,) * len(shape))


def token_spec(tile, width, first=0):
    at = first // tile
    return pl.BlockSpec((tile, width), lambda i: (i + at, 0))


def layer_spec(layer, rows, width):
    return pl.BlockSpec((None, rows, width), lambda i: (layer, 0, 0))


CHUNKS = 2
FORWARD_TILE = 256
BACKWARD_TILE = 256


def run_first(first, lat, order, blocks, start, wt, output_weight, norm_gain_table):
    size, width = start.shape
    tile = min(FORWARD_TILE, size)
    struct = jax.ShapeDtypeStruct
    part = struct((size, width), BF16)
    tok_spec = token_spec(tile, width)
    feat_spec = pl.BlockSpec((width, tile), lambda i: (0, i))
    at = first // tile
    return call(
        first_kernel,
        (
            struct((width, size), BF16),
            struct((6, 2 * width, size), BF16),
            struct((6, 8, size), F32),
            struct((width, size), BF16),
            part,
            part,
            *[struct((32, width), BF16)] * 3,
        ),
        grid=(size // tile,),
        in_specs=[scalar(), pl.BlockSpec((1, tile), lambda i: (0, i + at))]
        + [tok_spec] * 7
        + [
            layer_spec(0, 3 * width, width),
            layer_spec(0, width, width),
            fixed((2, width)),
        ],
        out_specs=(
            feat_spec,
            pl.BlockSpec((6, 2 * width, tile), lambda i: (0, 0, i)),
            pl.BlockSpec((6, 8, tile), lambda i: (0, 0, i)),
            feat_spec,
            tok_spec,
            tok_spec,
            *[fixed((32, width))] * 3,
        ),
        scratch=[pltpu.VMEM((6, 8, tile), F32), pltpu.VMEM((96, width), F32)],
        mib=LARGE_MIB,
        us=8,
    )(lat, order, *blocks, start, wt, output_weight, norm_gain_table)


def run_second(lat, places, normals, halos, query_key_value_weight, output_weight, cot):
    points, width = cot.shape
    struct = jax.ShapeDtypeStruct
    ext, slots = points + 64, points // 8
    across = pltpu.VMEM((width, points), BF16)
    every, halo = pltpu.VMEM((points, width), BF16), pltpu.VMEM((HALO, width), BF16)
    return call(
        second_kernel,
        (
            struct((points, 2 * width), BF16),
            struct((4 * width, width), BF16),
            struct((32, width), BF16),
            struct((48, width), BF16),
            struct((48, width), BF16),
        ),
        in_specs=[scalar()] + [whole()] * 11,
        out_specs=(whole(),) * 5,
        scratch=[
            across, every, every, across,
            *[halo] * 3,
            every,
            pltpu.VMEM((ext, width), BF16),
            pltpu.VMEM((ext, width), BF16),
            *[pltpu.VMEM((slots, width), BF16)] * 2,
            pltpu.VMEM((ext, width), F32),
            pltpu.VMEM((ext, width), F32),
            *[pltpu.VMEM((slots, width), BF16)] * 2,
            every,
            pltpu.VMEM((KEYS, 256), jnp.int32),
            every,
        ],
        mib=LARGE_MIB,
        us=22,
    )(lat, places, *normals, *halos, query_key_value_weight, output_weight, cot)


def inner_third_kernel(*refs):
    third_kernel(*refs[:14], None, *refs[14:17], None, *refs[17:25], None, *refs[25:])


def run_third(
    first, lat, order, blocks, kept, both, packs, wt, output_weight, norm_gain_table, weights
):
    q0, kv0, p0, mixed0, h1 = kept
    size, width = h1.shape
    points = both.shape[0]
    tile = min(BACKWARD_TILE, size)
    struct = jax.ShapeDtypeStruct
    part = struct((size, width), BF16)
    tok_spec = token_spec(tile, width)
    feat_spec = pl.BlockSpec((width, tile), lambda i: (0, i))
    final = packs is not None
    whole_dw, half_dw = (4 * width, width), (2 * width, width)
    return call(
        third_kernel if final else inner_third_kernel,
        (
            struct((size, width), F32),
            struct((size, width), F32),
            *[part] * 5,
            *([struct(half_dw, BF16)] * 2 if final else [struct(whole_dw, F32)]),
        ),
        grid=(size // tile,),
        in_specs=[scalar(), token_spec(tile, 1, first)]
        + [tok_spec] * 6
        + [
            feat_spec,
            pl.BlockSpec((6, 2 * width, tile), lambda i: (0, 0, i)),
            pl.BlockSpec((6, 8, tile), lambda i: (0, 0, i)),
            feat_spec,
            tok_spec,
        ]
        + [fixed((points, 2 * width))]
        + [fixed((RETURNED, width))] * final
        + [
            layer_spec(0, 3 * width, width),
            layer_spec(0, width, width),
            fixed((2, width)),
        ]
        + [fixed(whole_dw)] * final,
        out_specs=(*[tok_spec] * 7, *([fixed(half_dw)] * 2 if final else [fixed(whole_dw)])),
        scratch=[
            pltpu.VMEM(whole_dw, F32),
            pltpu.VMEM((width, tile), F32),
            pltpu.VMEM((2 * width, 6 * tile), BF16),
            pltpu.VMEM((width, tile), BF16),
            pltpu.VMEM((8, tile), F32),
            pltpu.VMEM((6 * tile, width), BF16),
        ],
        mib=LARGE_MIB,
        us=13,
    )(
        lat, order, *blocks, q0, kv0, p0, mixed0, h1, both, *([packs] if final else []), wt,
        output_weight, norm_gain_table, *([weights] if final else []),
    )


def local(
    tokens, visible, mask_token, norm_gain_table, query_key_value_weight, output_weight, cotangent
):
    rows, cols, width = tokens.shape
    points = rows * cols
    size = points // CHUNKS
    firsts = [c * size for c in range(CHUNKS)]
    lat_count, lon_count = lax.axis_size("lat"), lax.axis_size("lon")
    lat = lax.axis_index("lat").astype(jnp.int32).reshape(1)
    wt = jnp.swapaxes(query_key_value_weight, 1, 2)
    struct = jax.ShapeDtypeStruct
    tokens = tokens.reshape(points, width)
    cot = cotangent.reshape(points, width)
    part = struct((size, width), BF16)
    gain_spec = fixed((2, width))
    wt_spec, wo_spec = layer_spec(0, 3 * width, width), layer_spec(0, width, width)

    order, places = token_order(rows, cols)
    order_row = jnp.asarray(order.reshape(1, points))
    order, places = jnp.asarray(order.reshape(points, 1)), jnp.asarray(places.reshape(points, 1))

    small = 512
    starts, normals = [], []
    for first in firsts:
        start, normal = call(
            start_kernel,
            (part, part),
            grid=(size // small,),
            in_specs=[
                token_spec(small, 1, first),
                fixed((points, width)),
                fixed((rows, cols)),
                fixed((width,)),
                gain_spec,
            ],
            out_specs=(token_spec(small, width),) * 2,
            mib=LARGE_MIB,
            us=2,
        )(order, tokens, visible, mask_token, norm_gain_table)
        starts.append(start)
        normals.append(normal)

    swapped0 = lon_swap(normals[0])
    own1, swapped0, wt = lax.optimization_barrier((normals[1], swapped0, wt))
    swapped1 = lon_swap(own1)
    beyond0, beyond1 = lon_forward(swapped0), lon_forward(swapped1)
    near0, near1 = lat_swap(normals[0]), lat_swap(own1)

    def blocks_of(own, near, swapped, beyond):
        return [own, near, swapped, beyond, lat_swap(swapped), lat_swap(beyond)]

    blocks = [blocks_of(normals[0], near0, swapped0, beyond0), None]

    kept = []
    for c in range(CHUNKS):
        *keep, normal1, row, left, right = run_first(
            firsts[c], lat, order_row, blocks[c], starts[c], wt, output_weight, norm_gain_table
        )
        if c == 1:
            keep, normal1, halos = lax.optimization_barrier((keep, normal1, halos))
            halos = [*halos, lat_swap(halos[1]), lat_swap(halos[2])]
        kept.append((keep, normal1))
        if c == 0:
            beyond1, row, left, right = lax.optimization_barrier((beyond1, row, left, right))
            halos = [lat_swap(row), from_left(right), from_right(left)]
            blocks[1] = blocks_of(own1, near1, swapped1, beyond1)

    both1, dw1, brow, bleft, bright = run_second(
        lat, places, [kept[0][1], kept[1][1]], halos, query_key_value_weight, output_weight, cot
    )

    from_l, from_r, brow = from_left(bright), from_right(bleft), lat_swap(brow)
    stages = lon_factors()
    sum1 = halves_summed(
        lax.dynamic_slice_in_dim(dw1, lat[0] * 2 * width, 2 * width, 0),
        lax.dynamic_slice_in_dim(dw1, (1 - lat[0]) * 2 * width, 2 * width, 0),
    )
    both1, sum1 = chained(both1, sum1)
    border = (brow, from_l, from_r)

    def plus(a, b):
        return (a.astype(F32) + b.astype(F32)).astype(BF16)

    weights = packs = None
    sum_stages = list(stages)
    ends = []
    coming = returned = None
    for n, c in enumerate(range(CHUNKS)[::-1]):
        dh1, d0, d1, d2, d3, d4, d5, *weights = run_third(
            firsts[c], lat, order, blocks[c], kept[c][0], both1, packs, wt,
            output_weight, norm_gain_table, weights,
        )
        if n == 0:
            sum1 = stage_summed(sum1, sum_stages.pop(0))
        border, weights, sum1, d1, d2, d3, d4, d5, coming, returned = lax.optimization_barrier(
            (border, weights, sum1, d1, d2, d3, d4, d5, coming, returned)
        )
        if n == 0:
            brow, from_l, from_r = border
            packs = jnp.concatenate([brow, from_l, from_r, lat_swap(from_l), lat_swap(from_r)], 0)
        d3 = plus(d3, lat_swap(d5))
        d2 = plus(d2, lat_swap(d4))
        d1 = lat_swap(d1)
        if n == CHUNKS - 1:
            weights = [halves_summed(*weights)]
        weights, d1, d2, d3 = lax.optimization_barrier((weights, d1, d2, d3))
        if returned is not None:
            ends[-2][-1] = returned
        returned = None
        if coming is not None:
            returned = lon_swap(coming)
        coming = plus(d2, lon_backward(d3))
        weights = weights[0]
        ends.append([c, dh1, d0, d1, None])

    sum0 = stage_summed(weights, stages[0])
    for stage in sum_stages:
        sum1 = stage_summed(sum1, stage)
    sum0, sum1, coming, returned = lax.optimization_barrier((sum0, sum1, coming, returned))
    ends[-2][-1] = returned
    returned = lon_swap(coming)
    sum0 = stage_summed(sum0, stages[1])
    sum0, returned = lax.optimization_barrier((sum0, returned))
    ends[-1][-1] = returned
    for stage in stages[2:]:
        sum0 = stage_summed(sum0, stage)
    sums = jnp.concatenate([sum0, sum1], 0)
    for stage in stages[::-1]:
        sums = spread(sums, *stage)

    pieces = []
    for c, dh1, d0, near, far in ends:
        pieces.append((c, [starts[c], dh1, d0, far, near]))
    pieces = [array for _, arrays in sorted(pieces, key=lambda p: p[0]) for array in arrays]
    grad_tokens = call(
        last_kernel,
        struct((points, width), F32),
        in_specs=[whole()] * (4 + len(pieces)),
        out_specs=whole(),
        scratch=[pltpu.VMEM((points, width), BF16)] * 2,
        mib=LARGE_MIB,
        us=6,
    )(places, visible, norm_gain_table, cot, *pieces)
    sums, grad_tokens = chained(sums, grad_tokens)
    other = lat_swap(sums)
    factor = (points * lat_count * lon_count) ** (-0.5)
    g_qkv, g_out, g_gain = call(
        functools.partial(weights_kernel, factor, lon_count),
        (
            struct((2, width, 3 * width), F32),
            struct((2, width, width), F32),
            struct((2, width), F32),
        ),
        in_specs=[scalar()] + [whole()] * 4,
        out_specs=(whole(),) * 3,
        scratch=[pltpu.VMEM((2, 4 * width, width), F32)],
        mib=20,
        us=5,
    )(lat, sums, other, wt, norm_gain_table)
    return grad_tokens.reshape(rows, cols, width), g_qkv, g_out, g_gain


def without(kernel, at, count, *refs):
    kernel(*refs[:at], *[None] * count, *refs[at:])


def solution(mesh):
    return jax.shard_map(
        local,
        mesh=mesh,
        in_specs=(
            P(("group", "lat"), "lon", None),
            P(("group", "lat"), "lon"),
            P(),
            P(),
            P(),
            P(),
            P(("group", "lat"), "lon", None),
        ),
        out_specs=(
            P(("group", "lat"), "lon", None),
            P("group", None, None),
            P("group", None, None),
            P("group", None),
        ),
        check_vma=False,
    )
```

profile of v0, /device:TPU:0, one launch (start us, length us, event | category | flops | bytes accessed | tf_op | source)
XLA Modules:
  0.0 187.4 jit_solution(18233318960072819245)
XLA Ops:
  0.6 3.2 %shard_map.129 = (bf16[512,384]{1,0:T(8,128)(2,1)}, bf16[512,384]{1,0:T(8,128)(2,1)}) custom-call(s32[1024,1]{1,0:T(8,128)} %constant.91.clone.order_ref.refs_1_, bf16[1024,384]{1,0:T(8,128)(2,1)} %bitcast.12, s32[32,32]{1,0:T(8,128)} %vis_ref.5, bf16[384]{0:T(512)(128)(2,1)} %mask_ref.3, f32[2,384]{1,0:T(2,128)} %gain_ref.13), custom_call_target="tpu_custom_call" | custom-call | flops 1600000000 | bytes 2000000 | tf_op jit(solution)/shard_map/pallas_call | solution.py:702
  3.8 3.0 %collective-permute-start.1 = (bf16[512,384]{1,0:T(8,128)(2,1)}, bf16[512,384]{1,0:T(8,128)(2,1)S(1)}, u32[]{:S(2)}, u32[]{:S(2)}) collective-permute-start(bf16[512,384]{1,0:T(8,128)(2,1)} %get-tuple-element.101.n0), channel_id=1, source_target_pairs={{0,2},{2,0},{4,6},{6,4},{8,10},{10,8},{12,14},{14,12},{1,3},{3,1},... | collective-permute-start | bytes 1179656 | tf_op jit(solution)/shard_map/ppermute | solution.py:48
  6.8 2.3 %copy.14 = bf16[2,384,1152]{1,2,0:T(8,128)(2,1)} copy(bf16[2,384,1152]{2,1,0:T(8,128)(2,1)S(1)} %copy-done.2) | data formatting | bytes 3538944 | tf_op args[4]
  9.1 3.1 %shard_map.130 = (bf16[512,384]{1,0:T(8,128)(2,1)}, bf16[512,384]{1,0:T(8,128)(2,1)}) custom-call(s32[1024,1]{1,0:T(8,128)} %constant.91.clone.order_ref.refs_1_, bf16[1024,384]{1,0:T(8,128)(2,1)} %bitcast.13, s32[32,32]{1,0:T(8,128)} %vis_ref.5, bf16[384]{0:T(512)(128)(2,1)} %mask_ref.3, f32[2,384]{1,0:T(2,128)} %gain_ref.13), custom_call_target="tpu_custom_call" | custom-call | flops 1600000000 | bytes 2000000 | tf_op jit(solution)/shard_map/pallas_call | solution.py:702
  12.2 3.9 %collective-permute-done.1.n2 = bf16[512,384]{1,0:T(8,128)(2,1)S(1)} collective-permute-done((bf16[512,384]{1,0:T(8,128)(2,1)}, bf16[512,384]{1,0:T(8,128)(2,1)S(1)}, u32[]{:S(2)}, u32[]{:S(2)}) %collective-permute-start.1) | collective-permute-done | bytes 393248 | tf_op jit(solution)/shard_map/ppermute | solution.py:48
  17.9 3.5 %collective-permute-start.6 = (bf16[512,384]{1,0:T(8,128)(2,1)}, bf16[512,384]{1,0:T(8,128)(2,1)S(1)}, u32[]{:S(2)}, u32[]{:S(2)}) collective-permute-start(bf16[512,384]{1,0:T(8,128)(2,1)} %get-tuple-element.107.n0.refs_2_), channel_id=1, source_target_pairs={{0,2},{2,0},{4,6},{6,4},{8,10},{10,8},{12,14},{14,12},{1,3},{3,1},... | collective-permute-start | bytes 1179656 | tf_op jit(solution)/shard_map/ppermute | solution.py:48
  22.0 6.2 %collective-permute-done.2.n3 = bf16[512,384]{1,0:T(8,128)(2,1)S(1)} collective-permute-done((bf16[512,384]{1,0:T(8,128)(2,1)S(1)}, bf16[512,384]{1,0:T(8,128)(2,1)S(1)}, u32[]{:S(2)}, u32[]{:S(2)}) %collective-permute-start.2) | collective-permute-done | bytes 393248 | tf_op jit(solution)/shard_map/ppermute | solution.py:48
  31.2 8.5 %shard_map.131 = (bf16[384,512]{1,0:T(8,128)(2,1)}, bf16[6,768,512]{2,1,0:T(8,128)(2,1)}, f32[6,8,512]{2,1,0:T(8,128)}, bf16[384,512]{1,0:T(8,128)(2,1)}, bf16[5...) custom-call(s32[1]{0:T(128)} %bitcast.lat_ref.refs_0_, ...), custom_call_target="tpu_custom_call" | custom-call | flops 6400000000 | bytes 8000000 | tf_op jit(solution)/shard_map/pallas_call | solution.py:548
  39.7 1.9 collective-permute-done.7.n3.refs_5_
  42.1 1.8 collective-permute-start.11
  43.9 2.9 %collective-permute-start.12 = (bf16[32,384]{1,0:T(8,128)(2,1)}, bf16[32,384]{1,0:T(8,128)(2,1)S(1)}, u32[]{:S(2)}, u32[]{:S(2)}) collective-permute-start(bf16[32,384]{1,0:T(8,128)(2,1)} %get-tuple-element.121), channel_id=1, source_target_pairs={{0,14},{2,0},{4,2},{6,4},{8,6},{10,8},{12,10},{14,12},{1,15},{3,1}... | collective-permute-start | bytes 73736 | tf_op jit(solution)/shard_map/ppermute | solution.py:48
  47.8 8.6 %shard_map.132 = (bf16[384,512]{1,0:T(8,128)(2,1)}, bf16[6,768,512]{2,1,0:T(8,128)(2,1)}, f32[6,8,512]{2,1,0:T(8,128)}, bf16[384,512]{1,0:T(8,128)(2,1)}, bf16[5...) custom-call(s32[1]{0:T(128)} %bitcast.lat_ref.refs_0_, ...), custom_call_target="tpu_custom_call" | custom-call | flops 6400000000 | bytes 8000000 | tf_op jit(solution)/shard_map/pallas_call | solution.py:548
  58.5 22.0 %shard_map.133 = (bf16[1024,768]{1,0:T(8,128)(2,1)}, bf16[1536,384]{1,0:T(8,128)(2,1)}, bf16[32,384]{1,0:T(8,128)(2,1)}, bf16[48,384]{1,0:T(8,128)(2,1)}, bf16[48,384]{1,0:T(8,128)(2,1)}) custom-call(s32[1]{0:T(128)} %bitcast.lat_ref.refs_0_, s32[1024,1]{1,0:T(8,128)} %constant.92.clone.place_ref, bf16[512,384]{1,0:T(8,128)(2,1)} %get-tuple-element.106.na_ref, ...), custom_call_target="tpu_custom_call" | custom-call | flops 17600000000 | bytes 22000000 | tf_op jit(solution)/shard_map/pallas_call | solution.py:588
  82.1 4.7 %collective-permute-start.17 = (bf16[48,384]{1,0:T(8,128)(2,1)S(1)}, bf16[48,384]{1,0:T(8,128)(2,1)S(1)}, u32[]{:S(2)}, u32[]{:S(2)}) collective-permute-start(bf16[48,384]{1,0:T(8,128)(2,1)S(1)} %copy-done.26), channel_id=1, source_target_pairs={{0,14},{2,0},{4,2},{6,4},{8,6},{10,8},{12,10},{14,12},{1,15},{3,1}... | collective-permute-start | bytes 110600 | tf_op jit(solution)/shard_map/ppermute | solution.py:48
  87.1 15.0 %shard_map.134 = (f32[512,384]{1,0:T(8,128)}, f32[512,384]{1,0:T(8,128)}, bf16[512,384]{1,0:T(8,128)(2,1)}, bf16[512,384]{1,0:T(8,128)(2,1)}, bf16[512,384]{1,0:...) custom-call(s32[1]{0:T(128)} %bitcast.lat_ref.refs_0_, ...), custom_call_target="tpu_custom_call" | custom-call | flops 10400000000 | bytes 13000000 | tf_op jit(solution)/shard_map/pallas_call | solution.py:635
  106.0 16.0 %shard_map.135 = (f32[512,384]{1,0:T(8,128)}, f32[512,384]{1,0:T(8,128)}, bf16[512,384]{1,0:T(8,128)(2,1)}, bf16[512,384]{1,0:T(8,128)(2,1)}, bf16[512,384]{1,0:...) custom-call(s32[1]{0:T(128)} %bitcast.lat_ref.refs_0_, ...), custom_call_target="tpu_custom_call" | custom-call | flops 10400000000 | bytes 13000000 | tf_op jit(solution)/shard_map/pallas_call | solution.py:635
  125.9 3.0 %collective-permute-start.33 = (bf16[96,384]{1,0:T(8,128)(2,1)S(1)}, bf16[96,384]{1,0:T(8,128)(2,1)}, u32[]{:S(2)}, u32[]{:S(2)}) collective-permute-start(bf16[96,384]{1,0:T(8,128)(2,1)S(1)} %get-tuple-element.202), channel_id=1, source_target_pairs={{0,12},{2,14},{4,8},{6,10},{8,4},{10,6},{12,0},{14,2},{1,13},{3,15... | collective-permute-start | bytes 221192 | tf_op jit(solution)/shard_map/ppermute | solution.py:85
  130.0 1.9 %collective-permute-start.30 = (bf16[384,384]{1,0:T(8,128)(2,1)S(1)}, bf16[384,384]{1,0:T(8,128)(2,1)S(1)}, u32[]{:S(2)}, u32[]{:S(2)}) collective-permute-start(bf16[384,384]{1,0:T(8,128)(2,1)S(1)} %constant_dynamic-slice_fusion.6), channel_id=1, source_target_pairs={{0,2},{2,0},{4,6},{6,4},{8,10},{10,8},{12,14},{14,12},{1,3},{3,1},... | collective-permute-start | bytes 884744 | tf_op jit(solution)/shard_map/ppermute | solution.py:85
  132.1 3.1 %collective-permute-start.34 = (bf16[512,384]{1,0:T(8,128)(2,1)S(1)}, bf16[512,384]{1,0:T(8,128)(2,1)S(1)}, u32[]{:S(2)}, u32[]{:S(2)}) collective-permute-start(bf16[512,384]{1,0:T(8,128)(2,1)S(1)} %add_convert_fusion.3), channel_id=1, source_target_pairs={{0,12},{2,6},{4,0},{6,10},{8,4},{10,14},{12,8},{14,2},{1,13},{3,7}... | collective-permute-start | bytes 1179656 | tf_op jit(solution)/shard_map/ppermute | solution.py:48
  136.2 3.8 %collective-permute-done.30 = bf16[384,384]{1,0:T(8,128)(2,1)S(1)} collective-permute-done((bf16[384,384]{1,0:T(8,128)(2,1)S(1)}, bf16[384,384]{1,0:T(8,128)(2,1)S(1)}, u32[]{:S(2)}, u32[]{:S(2)}) %collective-permute-start.30) | collective-permute-done | bytes 294944 | tf_op jit(solution)/shard_map/ppermute | solution.py:85
  140.0 2.7 %collective-permute-done.34 = bf16[512,384]{1,0:T(8,128)(2,1)S(1)} collective-permute-done((bf16[512,384]{1,0:T(8,128)(2,1)S(1)}, bf16[512,384]{1,0:T(8,128)(2,1)S(1)}, u32[]{:S(2)}, u32[]{:S(2)}) %collective-permute-start.34) | collective-permute-done | bytes 393248 | tf_op jit(solution)/shard_map/ppermute | solution.py:48
  142.8 4.6 %collective-permute-done.35.refs_8_ = bf16[512,384]{1,0:T(8,128)(2,1)S(1)} collective-permute-done((bf16[512,384]{1,0:T(8,128)(2,1)S(1)}, bf16[512,384]{1,0:T(8,128)(2,1)S(1)}, u32[]{:S(2)}, u32[]{:S(2)}) %collective-permute-start.35) | collective-permute-done | bytes 393248 | tf_op jit(solution)/shard_map/ppermute | solution.py:48
  149.8 2.5 %collective-permute-start.37 = (bf16[96,384]{1,0:T(8,128)(2,1)S(1)}, bf16[96,384]{1,0:T(8,128)(2,1)S(1)}, u32[]{:S(2)}, u32[]{:S(2)}) collective-permute-start(bf16[96,384]{1,0:T(8,128)(2,1)S(1)} %get-tuple-element.200), channel_id=1, source_target_pairs={{0,8},{2,10},{4,12},{6,14},{8,0},{10,2},{12,4},{14,6},{1,9},{3,11}... | collective-permute-start | bytes 221192 | tf_op jit(solution)/shard_map/ppermute | solution.py:85
  153.6 2.9 %collective-permute-done.37 = bf16[96,384]{1,0:T(8,128)(2,1)S(1)} collective-permute-done((bf16[96,384]{1,0:T(8,128)(2,1)S(1)}, bf16[96,384]{1,0:T(8,128)(2,1)S(1)}, u32[]{:S(2)}, u32[]{:S(2)}) %collective-permute-start.37) | collective-permute-done | bytes 73760 | tf_op jit(solution)/shard_map/ppermute | solution.py:85
  156.6 1.9 %collective-permute-done.38 = bf16[96,384]{1,0:T(8,128)(2,1)S(1)} collective-permute-done((bf16[96,384]{1,0:T(8,128)(2,1)S(1)}, bf16[96,384]{1,0:T(8,128)(2,1)S(1)}, u32[]{:S(2)}, u32[]{:S(2)}) %collective-permute-start.38) | collective-permute-done | bytes 73760 | tf_op jit(solution)/shard_map/ppermute | solution.py:85
  158.7 1.9 %collective-permute-start.41 = (bf16[192,384]{1,0:T(8,128)(2,1)S(1)}, bf16[192,384]{1,0:T(8,128)(2,1)S(1)}, u32[]{:S(2)}, u32[]{:S(2)}) collective-permute-start(bf16[192,384]{1,0:T(8,128)(2,1)S(1)} %constant_dynamic-update-slice_fusion.5), channel_id=1, source_target_pairs={{0,8},{2,10},{4,12},{6,14},{8,0},{10,2},{12,4},{14,6},{1,9},{3,11}... | collective-permute-start | bytes 442376 | tf_op jit(solution)/shard_map/ppermute | solution.py:105
  160.6 2.4 %collective-permute-start.42 = (bf16[192,384]{1,0:T(8,128)(2,1)S(1)}, bf16[192,384]{1,0:T(8,128)(2,1)S(1)}, u32[]{:S(2)}, u32[]{:S(2)}) collective-permute-start(bf16[192,384]{1,0:T(8,128)(2,1)S(1)} %constant_dynamic-update-slice_fusion.5), channel_id=1, source_target_pairs={{0,12},{2,14},{4,8},{6,10},{8,4},{10,6},{12,0},{14,2},{1,13},{3,15... | collective-permute-start | bytes 442376 | tf_op jit(solution)/shard_map/ppermute | solution.py:105
  163.1 3.2 %collective-permute-done.40 = bf16[192,384]{1,0:T(8,128)(2,1)S(1)} collective-permute-done((bf16[192,384]{1,0:T(8,128)(2,1)S(1)}, bf16[192,384]{1,0:T(8,128)(2,1)S(1)}, u32[]{:S(2)}, u32[]{:S(2)}) %collective-permute-start.40) | collective-permute-done | bytes 147488 | tf_op jit(solution)/shard_map/ppermute | solution.py:105
  166.3 4.5 %collective-permute-done.41 = bf16[192,384]{1,0:T(8,128)(2,1)S(1)} collective-permute-done((bf16[192,384]{1,0:T(8,128)(2,1)S(1)}, bf16[192,384]{1,0:T(8,128)(2,1)S(1)}, u32[]{:S(2)}, u32[]{:S(2)}) %collective-permute-start.41) | collective-permute-done | bytes 147488 | tf_op jit(solution)/shard_map/ppermute | solution.py:105
  172.1 8.0 %shard_map.136 = f32[1024,384]{1,0:T(8,128)} custom-call(s32[1024,1]{1,0:T(8,128)} %constant.92.clone.place_ref, s32[32,32]{1,0:T(8,128)} %vis_ref.5, f32[2,384]{1,0:T(2,128)} %gain_ref.13, f32[1024,384]{1,0:T(8,128)} %bitcast.11, bf16[512,384]{1,0:T(8,128)(2,1)} %get-tuple-element.104.start_ref.refs_0_, f32[512,384]{1,0:T(8,128)} %get-tuple-element.185.refs_1_, ...), custom_call_target="tpu_custom_call" | custom-call | flops 4800000000 | bytes 6000000 | tf_op jit(solution)/shard_map/pallas_call | solution.py:812
  181.0 2.8 %collective-permute-done.44.other_ref = bf16[1536,384]{1,0:T(8,128)(2,1)S(1)} collective-permute-done((bf16[1536,384]{1,0:T(8,128)(2,1)S(1)}, bf16[1536,384]{1,0:T(8,128)(2,1)S(1)}, u32[]{:S(2)}, u32[]{:S(2)}) %collective-permute-start.44) | collective-permute-done | bytes 1179680 | tf_op jit(solution)/shard_map/ppermute | solution.py:48
  183.8 3.6 %shard_map.137 = (f32[2,384,1152]{2,1,0:T(8,128)}, f32[2,384,384]{2,1,0:T(8,128)}, f32[2,384]{1,0:T(2,128)}) custom-call(s32[1]{0:T(128)} %bitcast.lat_ref.refs_0_, bf16[1536,384]{1,0:T(8,128)(2,1)S(1)} %constant_dynamic-update-slice_fusion.7.mine_ref, bf16[1536,384]{1,0:T(8,128)(2,1)S(1)} %collective-permute-done.44.other_ref, ...), custom_call_target="tpu_custom_call" | custom-call | flops 4000000000 | bytes 5000000 | tf_op jit(solution)/shard_map/pallas_call | solution.py:824
  (164 shorter events, 26.6 us)
Async XLA Ops:
  3.8 12.3 %collective-permute-start.1 = (bf16[512,384]{1,0:T(8,128)(2,1)}, bf16[512,384]{1,0:T(8,128)(2,1)S(1)}, u32[]{:S(2)}, u32[]{:S(2)}) collective-permute-start(bf16[512,384]{1,0:T(8,128)(2,1)} %get-tuple-element.101.n0), channel_id=1, source_target_pairs={{0,2},{2,0},{4,6},{6,4},{8,10},{10,8},{12,14},{14,12},{1,3},{3,1},... | collective-permute-start | bytes 1179656 | tf_op jit(solution)/shard_map/ppermute | solution.py:48
  16.1 12.1 %collective-permute-start.2 = (bf16[512,384]{1,0:T(8,128)(2,1)S(1)}, bf16[512,384]{1,0:T(8,128)(2,1)S(1)}, u32[]{:S(2)}, u32[]{:S(2)}) collective-permute-start(bf16[512,384]{1,0:T(8,128)(2,1)S(1)} %collective-permute-done.1.n2), channel_id=1, source_target_pairs={{0,4},{2,14},{4,8},{6,2},{8,12},{10,6},{12,0},{14,10},{1,5},{3,15}... | collective-permute-start | bytes 1179656 | tf_op jit(solution)/shard_map/ppermute | solution.py:48
  17.9 11.7 %collective-permute-start.6 = (bf16[512,384]{1,0:T(8,128)(2,1)}, bf16[512,384]{1,0:T(8,128)(2,1)S(1)}, u32[]{:S(2)}, u32[]{:S(2)}) collective-permute-start(bf16[512,384]{1,0:T(8,128)(2,1)} %get-tuple-element.107.n0.refs_2_), channel_id=1, source_target_pairs={{0,2},{2,0},{4,6},{6,4},{8,10},{10,8},{12,14},{14,12},{1,3},{3,1},... | collective-permute-start | bytes 1179656 | tf_op jit(solution)/shard_map/ppermute | solution.py:48
  21.5 8.2 %collective-permute-start = (bf16[512,384]{1,0:T(8,128)(2,1)S(1)}, bf16[512,384]{1,0:T(8,128)(2,1)S(1)}, u32[]{:S(2)}, u32[]{:S(2)}) collective-permute-start(bf16[512,384]{1,0:T(8,128)(2,1)S(1)} %copy-done.11), channel_id=1, source_target_pairs={{0,1},{1,0},{2,3},{3,2},{4,5},{5,4},{6,7},{7,6},{8,9},{9,8},{10,11... | collective-permute-start | bytes 1179656 | tf_op jit(solution)/shard_map/ppermute | solution.py:48
  21.5 8.3 %collective-permute-start.3 = (bf16[512,384]{1,0:T(8,128)(2,1)S(1)}, bf16[512,384]{1,0:T(8,128)(2,1)S(1)}, u32[]{:S(2)}, u32[]{:S(2)}) collective-permute-start(bf16[512,384]{1,0:T(8,128)(2,1)S(1)} %collective-permute-done.1.n2), channel_id=1, source_target_pairs={{0,1},{1,0},{2,3},{3,2},{4,5},{5,4},{6,7},{7,6},{8,9},{9,8},{10,11... | collective-permute-start | bytes 1179656 | tf_op jit(solution)/shard_map/ppermute | solution.py:48
  28.2 15.7 %collective-permute-start.5 = (bf16[512,384]{1,0:T(8,128)(2,1)}, bf16[512,384]{1,0:T(8,128)(2,1)S(1)}, u32[]{:S(2)}, u32[]{:S(2)}) collective-permute-start(bf16[512,384]{1,0:T(8,128)(2,1)} %get-tuple-element.107.n0.refs_2_), channel_id=1, source_target_pairs={{0,1},{1,0},{2,3},{3,2},{4,5},{5,4},{6,7},{7,6},{8,9},{9,8},{10,11... | collective-permute-start | bytes 1179656 | tf_op jit(solution)/shard_map/ppermute | solution.py:48
  29.6 12.0 %collective-permute-start.7 = (bf16[512,384]{1,0:T(8,128)(2,1)S(1)}, bf16[512,384]{1,0:T(8,128)(2,1)S(1)}, u32[]{:S(2)}, u32[]{:S(2)}) collective-permute-start(bf16[512,384]{1,0:T(8,128)(2,1)S(1)} %collective-permute-done.6.n2.refs_4_), channel_id=1, source_target_pairs={{0,4},{2,14},{4,8},{6,2},{8,12},{10,6},{12,0},{14,10},{1,5},{3,15}... | collective-permute-start | bytes 1179656 | tf_op jit(solution)/shard_map/ppermute | solution.py:48
  29.6 17.2 %collective-permute-start.8 = (bf16[512,384]{1,0:T(8,128)(2,1)S(1)}, bf16[512,384]{1,0:T(8,128)(2,1)S(1)}, u32[]{:S(2)}, u32[]{:S(2)}) collective-permute-start(bf16[512,384]{1,0:T(8,128)(2,1)S(1)} %collective-permute-done.6.n2.refs_4_), channel_id=1, source_target_pairs={{0,1},{1,0},{2,3},{3,2},{4,5},{5,4},{6,7},{7,6},{8,9},{9,8},{10,11... | collective-permute-start | bytes 1179656 | tf_op jit(solution)/shard_map/ppermute | solution.py:48
  41.6 5.2 %collective-permute-start.9 = (bf16[512,384]{1,0:T(8,128)(2,1)S(1)}, bf16[512,384]{1,0:T(8,128)(2,1)S(1)}, u32[]{:S(2)}, u32[]{:S(2)}) collective-permute-start(bf16[512,384]{1,0:T(8,128)(2,1)S(1)} %collective-permute-done.7.n3.refs_5_), channel_id=1, source_target_pairs={{0,1},{1,0},{2,3},{3,2},{4,5},{5,4},{6,7},{7,6},{8,9},{9,8},{10,11... | collective-permute-start | bytes 1179656 | tf_op jit(solution)/shard_map/ppermute | solution.py:48
  41.6 14.8 %collective-permute-start.10 = (bf16[32,384]{1,0:T(8,128)(2,1)}, bf16[32,384]{1,0:T(8,128)(2,1)S(1)}, u32[]{:S(2)}, u32[]{:S(2)}) collective-permute-start(bf16[32,384]{1,0:T(8,128)(2,1)} %get-tuple-element.119), channel_id=1, source_target_pairs={{0,1},{1,0},{2,3},{3,2},{4,5},{5,4},{6,7},{7,6},{8,9},{9,8},{10,11... | collective-permute-start | bytes 73736 | tf_op jit(solution)/shard_map/ppermute | solution.py:48
  42.1 14.3 %collective-permute-start.11 = (bf16[32,384]{1,0:T(8,128)(2,1)}, bf16[32,384]{1,0:T(8,128)(2,1)S(1)}, u32[]{:S(2)}, u32[]{:S(2)}) collective-permute-start(bf16[32,384]{1,0:T(8,128)(2,1)} %get-tuple-element.120), channel_id=1, source_target_pairs={{0,2},{2,4},{4,6},{6,8},{8,10},{10,12},{12,14},{14,0},{1,3},{3,5},... | collective-permute-start | bytes 73736 | tf_op jit(solution)/shard_map/ppermute | solution.py:48
  43.9 12.5 %collective-permute-start.12 = (bf16[32,384]{1,0:T(8,128)(2,1)}, bf16[32,384]{1,0:T(8,128)(2,1)S(1)}, u32[]{:S(2)}, u32[]{:S(2)}) collective-permute-start(bf16[32,384]{1,0:T(8,128)(2,1)} %get-tuple-element.121), channel_id=1, source_target_pairs={{0,14},{2,0},{4,2},{6,4},{8,6},{10,8},{12,10},{14,12},{1,15},{3,1}... | collective-permute-start | bytes 73736 | tf_op jit(solution)/shard_map/ppermute | solution.py:48
  82.1 20.1 %collective-permute-start.16 = (bf16[48,384]{1,0:T(8,128)(2,1)}, bf16[48,384]{1,0:T(8,128)(2,1)S(1)}, u32[]{:S(2)}, u32[]{:S(2)}) collective-permute-start(bf16[48,384]{1,0:T(8,128)(2,1)} %get-tuple-element.127), channel_id=1, source_target_pairs={{0,2},{2,4},{4,6},{6,8},{8,10},{10,12},{12,14},{14,0},{1,3},{3,5},... | collective-permute-start | bytes 110600 | tf_op jit(solution)/shard_map/ppermute | solution.py:48
  82.1 20.1 %collective-permute-start.17 = (bf16[48,384]{1,0:T(8,128)(2,1)S(1)}, bf16[48,384]{1,0:T(8,128)(2,1)S(1)}, u32[]{:S(2)}, u32[]{:S(2)}) collective-permute-start(bf16[48,384]{1,0:T(8,128)(2,1)S(1)} %copy-done.26), channel_id=1, source_target_pairs={{0,14},{2,0},{4,2},{6,4},{8,6},{10,8},{12,10},{14,12},{1,15},{3,1}... | collective-permute-start | bytes 110600 | tf_op jit(solution)/shard_map/ppermute | solution.py:48
  86.8 15.4 %collective-permute-start.15 = (bf16[32,384]{1,0:T(8,128)(2,1)}, bf16[32,384]{1,0:T(8,128)(2,1)S(1)}, u32[]{:S(2)}, u32[]{:S(2)}) collective-permute-start(bf16[32,384]{1,0:T(8,128)(2,1)} %get-tuple-element.126), channel_id=1, source_target_pairs={{0,1},{1,0},{2,3},{3,2},{4,5},{5,4},{6,7},{7,6},{8,9},{9,8},{10,11... | collective-permute-start | bytes 73736 | tf_op jit(solution)/shard_map/ppermute | solution.py:48
  87.1 15.1 %collective-permute-start.19 = (bf16[384,384]{1,0:T(8,128)(2,1)S(1)}, bf16[384,384]{1,0:T(8,128)(2,1)S(1)}, u32[]{:S(2)}, u32[]{:S(2)}) collective-permute-start(bf16[384,384]{1,0:T(8,128)(2,1)S(1)} %constant_dynamic-slice_fusion.7), channel_id=1, source_target_pairs={{0,2},{2,0},{4,6},{6,4},{8,10},{10,8},{12,14},{14,12},{1,3},{3,1},... | collective-permute-start | bytes 884744 | tf_op jit(solution)/shard_map/ppermute | solution.py:85
  105.6 16.5 %collective-permute-start.25 = (bf16[512,384]{1,0:T(8,128)(2,1)S(1)}, bf16[512,384]{1,0:T(8,128)(2,1)S(1)}, u32[]{:S(2)}, u32[]{:S(2)}) collective-permute-start(bf16[512,384]{1,0:T(8,128)(2,1)S(1)} %add_convert_fusion.6), channel_id=1, source_target_pairs={{0,12},{2,6},{4,0},{6,10},{8,4},{10,14},{12,8},{14,2},{1,13},{3,7}... | collective-permute-start | bytes 1179656 | tf_op jit(solution)/shard_map/ppermute | solution.py:48
  123.6 5.5 %collective-permute-start.26 = (bf16[768,384]{1,0:T(8,128)(2,1)}, bf16[768,384]{1,0:T(8,128)(2,1)S(1)}, u32[]{:S(2)}, u32[]{:S(2)}) collective-permute-start(bf16[768,384]{1,0:T(8,128)(2,1)} %get-tuple-element.170), channel_id=1, source_target_pairs={{0,1},{1,0},{2,3},{3,2},{4,5},{5,4},{6,7},{7,6},{8,9},{9,8},{10,11... | collective-permute-start | bytes 1769480 | tf_op jit(solution)/shard_map/ppermute | solution.py:48
  123.6 5.6 %collective-permute-start.27 = (bf16[512,384]{1,0:T(8,128)(2,1)}, bf16[512,384]{1,0:T(8,128)(2,1)S(1)}, u32[]{:S(2)}, u32[]{:S(2)}) collective-permute-start(bf16[512,384]{1,0:T(8,128)(2,1)} %get-tuple-element.171), channel_id=1, source_target_pairs={{0,1},{1,0},{2,3},{3,2},{4,5},{5,4},{6,7},{7,6},{8,9},{9,8},{10,11... | collective-permute-start | bytes 1179656 | tf_op jit(solution)/shard_map/ppermute | solution.py:48
  124.1 8.0 %collective-permute-start.31 = (bf16[96,384]{1,0:T(8,128)(2,1)S(1)}, bf16[96,384]{1,0:T(8,128)(2,1)S(1)}, u32[]{:S(2)}, u32[]{:S(2)}) collective-permute-start(bf16[96,384]{1,0:T(8,128)(2,1)S(1)} %get-tuple-element.201), channel_id=1, source_target_pairs={{0,4},{2,6},{4,0},{6,2},{8,12},{10,14},{12,8},{14,10},{1,5},{3,7},... | collective-permute-start | bytes 221192 | tf_op jit(solution)/shard_map/ppermute | solution.py:85
  125.8 9.4 %collective-permute-start.32 = (bf16[96,384]{1,0:T(8,128)(2,1)S(1)}, bf16[96,384]{1,0:T(8,128)(2,1)S(1)}, u32[]{:S(2)}, u32[]{:S(2)}) collective-permute-start(bf16[96,384]{1,0:T(8,128)(2,1)S(1)} %get-tuple-element.203), channel_id=1, source_target_pairs={{0,8},{2,10},{4,12},{6,14},{8,0},{10,2},{12,4},{14,6},{1,9},{3,11}... | collective-permute-start | bytes 221192 | tf_op jit(solution)/shard_map/ppermute | solution.py:85
  125.9 9.3 %collective-permute-start.33 = (bf16[96,384]{1,0:T(8,128)(2,1)S(1)}, bf16[96,384]{1,0:T(8,128)(2,1)}, u32[]{:S(2)}, u32[]{:S(2)}) collective-permute-start(bf16[96,384]{1,0:T(8,128)(2,1)S(1)} %get-tuple-element.202), channel_id=1, source_target_pairs={{0,12},{2,14},{4,8},{6,10},{8,4},{10,6},{12,0},{14,2},{1,13},{3,15... | collective-permute-start | bytes 221192 | tf_op jit(solution)/shard_map/ppermute | solution.py:85
  130.0 9.9 %collective-permute-start.30 = (bf16[384,384]{1,0:T(8,128)(2,1)S(1)}, bf16[384,384]{1,0:T(8,128)(2,1)S(1)}, u32[]{:S(2)}, u32[]{:S(2)}) collective-permute-start(bf16[384,384]{1,0:T(8,128)(2,1)S(1)} %constant_dynamic-slice_fusion.6), channel_id=1, source_target_pairs={{0,2},{2,0},{4,6},{6,4},{8,10},{10,8},{12,14},{14,12},{1,3},{3,1},... | collective-permute-start | bytes 884744 | tf_op jit(solution)/shard_map/ppermute | solution.py:85
  132.0 15.5 %collective-permute-start.35 = (bf16[512,384]{1,0:T(8,128)(2,1)S(1)}, bf16[512,384]{1,0:T(8,128)(2,1)S(1)}, u32[]{:S(2)}, u32[]{:S(2)}) collective-permute-start(bf16[512,384]{1,0:T(8,128)(2,1)S(1)} %add_convert_fusion.5), channel_id=1, source_target_pairs={{0,2},{2,0},{4,6},{6,4},{8,10},{10,8},{12,14},{14,12},{1,3},{3,1},... | collective-permute-start | bytes 1179656 | tf_op jit(solution)/shard_map/ppermute | solution.py:48
  132.1 10.6 %collective-permute-start.34 = (bf16[512,384]{1,0:T(8,128)(2,1)S(1)}, bf16[512,384]{1,0:T(8,128)(2,1)S(1)}, u32[]{:S(2)}, u32[]{:S(2)}) collective-permute-start(bf16[512,384]{1,0:T(8,128)(2,1)S(1)} %add_convert_fusion.3), channel_id=1, source_target_pairs={{0,12},{2,6},{4,0},{6,10},{8,4},{10,14},{12,8},{14,2},{1,13},{3,7}... | collective-permute-start | bytes 1179656 | tf_op jit(solution)/shard_map/ppermute | solution.py:48
  147.4 11.1 %collective-permute-start.39 = (bf16[512,384]{1,0:T(8,128)(2,1)S(1)}, bf16[512,384]{1,0:T(8,128)(2,1)S(1)}, u32[]{:S(2)}, u32[]{:S(2)}) collective-permute-start(bf16[512,384]{1,0:T(8,128)(2,1)S(1)} %add_convert_fusion.2), channel_id=1, source_target_pairs={{0,2},{2,0},{4,6},{6,4},{8,10},{10,8},{12,14},{14,12},{1,3},{3,1},... | collective-permute-start | bytes 1179656 | tf_op jit(solution)/shard_map/ppermute | solution.py:48
  149.8 6.8 %collective-permute-start.37 = (bf16[96,384]{1,0:T(8,128)(2,1)S(1)}, bf16[96,384]{1,0:T(8,128)(2,1)S(1)}, u32[]{:S(2)}, u32[]{:S(2)}) collective-permute-start(bf16[96,384]{1,0:T(8,128)(2,1)S(1)} %get-tuple-element.200), channel_id=1, source_target_pairs={{0,8},{2,10},{4,12},{6,14},{8,0},{10,2},{12,4},{14,6},{1,9},{3,11}... | collective-permute-start | bytes 221192 | tf_op jit(solution)/shard_map/ppermute | solution.py:85
  152.3 6.2 %collective-permute-start.38 = (bf16[96,384]{1,0:T(8,128)(2,1)S(1)}, bf16[96,384]{1,0:T(8,128)(2,1)S(1)}, u32[]{:S(2)}, u32[]{:S(2)}) collective-permute-start(bf16[96,384]{1,0:T(8,128)(2,1)S(1)} %get-tuple-element.199), channel_id=1, source_target_pairs={{0,12},{2,14},{4,8},{6,10},{8,4},{10,6},{12,0},{14,2},{1,13},{3,15... | collective-permute-start | bytes 221192 | tf_op jit(solution)/shard_map/ppermute | solution.py:85
  158.6 7.7 %collective-permute-start.40 = (bf16[192,384]{1,0:T(8,128)(2,1)S(1)}, bf16[192,384]{1,0:T(8,128)(2,1)S(1)}, u32[]{:S(2)}, u32[]{:S(2)}) collective-permute-start(bf16[192,384]{1,0:T(8,128)(2,1)S(1)} %constant_dynamic-update-slice_fusion.5), channel_id=1, source_target_pairs={{0,4},{2,6},{4,0},{6,2},{8,12},{10,14},{12,8},{14,10},{1,5},{3,7},... | collective-permute-start | bytes 442376 | tf_op jit(solution)/shard_map/ppermute | solution.py:105
  158.7 12.1 %collective-permute-start.41 = (bf16[192,384]{1,0:T(8,128)(2,1)S(1)}, bf16[192,384]{1,0:T(8,128)(2,1)S(1)}, u32[]{:S(2)}, u32[]{:S(2)}) collective-permute-start(bf16[192,384]{1,0:T(8,128)(2,1)S(1)} %constant_dynamic-update-slice_fusion.5), channel_id=1, source_target_pairs={{0,8},{2,10},{4,12},{6,14},{8,0},{10,2},{12,4},{14,6},{1,9},{3,11}... | collective-permute-start | bytes 442376 | tf_op jit(solution)/shard_map/ppermute | solution.py:105
  160.6 10.2 %collective-permute-start.42 = (bf16[192,384]{1,0:T(8,128)(2,1)S(1)}, bf16[192,384]{1,0:T(8,128)(2,1)S(1)}, u32[]{:S(2)}, u32[]{:S(2)}) collective-permute-start(bf16[192,384]{1,0:T(8,128)(2,1)S(1)} %constant_dynamic-update-slice_fusion.5), channel_id=1, source_target_pairs={{0,12},{2,14},{4,8},{6,10},{8,4},{10,6},{12,0},{14,2},{1,13},{3,15... | collective-permute-start | bytes 442376 | tf_op jit(solution)/shard_map/ppermute | solution.py:105
  170.8 9.9 %collective-permute-start.43 = (bf16[768,384]{1,0:T(8,128)(2,1)S(1)}, bf16[768,384]{1,0:T(8,128)(2,1)S(1)}, u32[]{:S(2)}, u32[]{:S(2)}) collective-permute-start(bf16[768,384]{1,0:T(8,128)(2,1)S(1)} %constant_dynamic-update-slice_fusion.9), channel_id=1, source_target_pairs={{0,2},{2,0},{4,6},{6,4},{8,10},{10,8},{12,14},{14,12},{1,3},{3,1},... | collective-permute-start | bytes 1769480 | tf_op jit(solution)/shard_map/ppermute | solution.py:105
  (45 other events, 175.8 us)
where the time goes:
time: 191 us; the launch traced here: 187 us
  Pallas kernels  88 us (46%)
  starting transfers between devices  45.3 us (24%)
  waiting for transfers between devices  42.8 us (22%)
  local copies, waits for them, and re-layouts  8.04 us (4%)
  other arithmetic  2.04 us (1%)
    pallas_call x2, Pallas kernels, run_third(): call(third_kernel if final else inner_third_kernel, (struct((size, width)...  30.9 us
    ppermute x33, starting transfers between devices, permuted(): lax.ppermute(value, axis, [(i, target(i) % count) for i in range(count)])  28.5 us
    ppermute x33, waiting for transfers between devices, permuted(): lax.ppermute(value, axis, [(i, target(i) % count) for i in range(count)])  26.1 us
    pallas_call x1, Pallas kernels, run_second(): call(second_kernel, (struct((points, 2 * width), BF16), struct((4 * width...  22 us
    pallas_call x2, Pallas kernels, run_first(): call(first_kernel, (struct((width, size), BF16), struct((6, 2 * width, si...  17.1 us
    ppermute x8, starting transfers between devices, exchanged(): moved.append(lax.ppermute(parts(digit ^ d), 'lon', pairs))  11.2 us
    ppermute x8, waiting for transfers between devices, exchanged(): moved.append(lax.ppermute(parts(digit ^ d), 'lon', pairs))  8.61 us
    ppermute x4, waiting for transfers between devices, spread(): got = lax.ppermute(value, 'lon', pairs)  8.08 us
  transfers between devices with their start and end apart: 45, of which 19 were waited for; matrix products, arithmetic and copies ran while one was open for 3% of the time, Pallas kernels for 32%

commit v1 on v0

--- a/solution.py
+++ b/solution.py
@@ -428,7 +428,7 @@
         n_s[b * tile : (b + 1) * tile, :] = ref[...]
     dw_s[width : 3 * width, :] += nn(dkv_s[...], n_s[...])
     grads = tn(dkv_s[...], wt_ref[width : 3 * width])
-    outs[0][...] = grads[0:tile] + tn(dq, wt_ref[0:width])
+    outs[0][...] = (grads[0:tile] + tn(dq, wt_ref[0:width])).astype(BF16)
     for b in range(1, len(blocks)):
         outs[b][...] = grads[b * tile : (b + 1) * tile].astype(BF16)
 
@@ -449,7 +449,7 @@
         start_ref, dh_ref, own_ref, far_ref, near_ref = inputs[:5]
         for lo in range(0, start_ref.shape[0], tile):
             rows = slice(lo, lo + tile)
-            dn = own_ref[rows] + far_ref[rows].astype(F32) + near_ref[rows].astype(F32)
+            dn = own_ref[rows].astype(F32) + far_ref[rows].astype(F32) + near_ref[rows].astype(F32)
             back = norm_back(start_ref[rows].astype(F32), gain_ref[0:1, :], dn)
             grad = dh_ref[rows] + back
             high = grad.astype(BF16)
@@ -636,8 +636,7 @@
         third_kernel if final else inner_third_kernel,
         (
             struct((size, width), F32),
-            struct((size, width), F32),
-            *[part] * 5,
+            *[part] * 6,
             *([struct(half_dw, BF16)] * 2 if final else [struct(whole_dw, F32)]),
         ),
         grid=(size // tile,),

time: 191 us -> 191 us (level)
  transfers between devices with their start and end apart: 45 -> 45, of which waited for: 19 -> 19; matrix products, arithmetic and copies ran while one was open for 3% -> 3% of each run, Pallas kernels for 32% -> 31%
where the time goes in v1:
time: 191 us; the launch traced here: 187 us
  Pallas kernels  87.6 us (46%)
  starting transfers between devices  45.4 us (24%)
  waiting for transfers between devices  42.9 us (22%)
  local copies, waits for them, and re-layouts  8.07 us (4%)
  other arithmetic  2.04 us (1%)
    pallas_call x2, Pallas kernels, run_third(): call(third_kernel if final else inner_third_kernel, (struct((size, width)...  30.7 us
    ppermute x33, starting transfers between devices, permuted(): lax.ppermute(value, axis, [(i, target(i) % count) for i in range(count)])  28.5 us
    ppermute x33, waiting for transfers between devices, permuted(): lax.ppermute(value, axis, [(i, target(i) % count) for i in range(count)])  26.1 us
    pallas_call x1, Pallas kernels, run_second(): call(second_kernel, (struct((points, 2 * width), BF16), struct((4 * width...  22 us
    pallas_call x2, Pallas kernels, run_first(): call(first_kernel, (struct((width, size), BF16), struct((6, 2 * width, si...  17.2 us
    ppermute x8, starting transfers between devices, exchanged(): moved.append(lax.ppermute(parts(digit ^ d), 'lon', pairs))  11.2 us
    ppermute x8, waiting for transfers between devices, exchanged(): moved.append(lax.ppermute(parts(digit ^ d), 'lon', pairs))  8.62 us
    ppermute x4, waiting for transfers between devices, spread(): got = lax.ppermute(value, 'lon', pairs)  8.23 us
  transfers between devices with their start and end apart: 45, of which 19 were waited for; matrix products, arithmetic and copies ran while one was open for 3% of the time, Pallas kernels for 31%

profile of v1, /device:TPU:0, one launch (start us, length us, event | category | flops | bytes accessed | tf_op | source)
XLA Modules:
  0.0 187.3 jit_solution(6310892674075955251)
XLA Ops:
  0.6 3.2 %shard_map.129 = (bf16[512,384]{1,0:T(8,128)(2,1)}, bf16[512,384]{1,0:T(8,128)(2,1)}) custom-call(s32[1024,1]{1,0:T(8,128)} %constant.91.clone.order_ref.refs_1_, bf16[1024,384]{1,0:T(8,128)(2,1)} %bitcast.12, s32[32,32]{1,0:T(8,128)} %vis_ref.5, bf16[384]{0:T(512)(128)(2,1)} %mask_ref.3, f32[2,384]{1,0:T(2,128)} %gain_ref.13), custom_call_target="tpu_custom_call" | custom-call | flops 1600000000 | bytes 2000000 | tf_op jit(solution)/shard_map/pallas_call | solution.py:701
  3.9 3.0 %collective-permute-start.1 = (bf16[512,384]{1,0:T(8,128)(2,1)}, bf16[512,384]{1,0:T(8,128)(2,1)S(1)}, u32[]{:S(2)}, u32[]{:S(2)}) collective-permute-start(bf16[512,384]{1,0:T(8,128)(2,1)} %get-tuple-element.101.n0), channel_id=1, source_target_pairs={{0,2},{2,0},{4,6},{6,4},{8,10},{10,8},{12,14},{14,12},{1,3},{3,1},... | collective-permute-start | bytes 1179656 | tf_op jit(solution)/shard_map/ppermute | solution.py:48
  6.8 2.3 %copy.14 = bf16[2,384,1152]{1,2,0:T(8,128)(2,1)} copy(bf16[2,384,1152]{2,1,0:T(8,128)(2,1)S(1)} %copy-done.2) | data formatting | bytes 3538944 | tf_op args[4]
  9.1 3.1 %shard_map.130 = (bf16[512,384]{1,0:T(8,128)(2,1)}, bf16[512,384]{1,0:T(8,128)(2,1)}) custom-call(s32[1024,1]{1,0:T(8,128)} %constant.91.clone.order_ref.refs_1_, bf16[1024,384]{1,0:T(8,128)(2,1)} %bitcast.13, s32[32,32]{1,0:T(8,128)} %vis_ref.5, bf16[384]{0:T(512)(128)(2,1)} %mask_ref.3, f32[2,384]{1,0:T(2,128)} %gain_ref.13), custom_call_target="tpu_custom_call" | custom-call | flops 1600000000 | bytes 2000000 | tf_op jit(solution)/shard_map/pallas_call | solution.py:701
  12.2 3.9 %collective-permute-done.1.n2 = bf16[512,384]{1,0:T(8,128)(2,1)S(1)} collective-permute-done((bf16[512,384]{1,0:T(8,128)(2,1)}, bf16[512,384]{1,0:T(8,128)(2,1)S(1)}, u32[]{:S(2)}, u32[]{:S(2)}) %collective-permute-start.1) | collective-permute-done | bytes 393248 | tf_op jit(solution)/shard_map/ppermute | solution.py:48
  17.9 3.5 %collective-permute-start.6 = (bf16[512,384]{1,0:T(8,128)(2,1)}, bf16[512,384]{1,0:T(8,128)(2,1)S(1)}, u32[]{:S(2)}, u32[]{:S(2)}) collective-permute-start(bf16[512,384]{1,0:T(8,128)(2,1)} %get-tuple-element.107.n0.refs_2_), channel_id=1, source_target_pairs={{0,2},{2,0},{4,6},{6,4},{8,10},{10,8},{12,14},{14,12},{1,3},{3,1},... | collective-permute-start | bytes 1179656 | tf_op jit(solution)/shard_map/ppermute | solution.py:48
  22.0 6.2 %collective-permute-done.2.n3 = bf16[512,384]{1,0:T(8,128)(2,1)S(1)} collective-permute-done((bf16[512,384]{1,0:T(8,128)(2,1)S(1)}, bf16[512,384]{1,0:T(8,128)(2,1)S(1)}, u32[]{:S(2)}, u32[]{:S(2)}) %collective-permute-start.2) | collective-permute-done | bytes 393248 | tf_op jit(solution)/shard_map/ppermute | solution.py:48
  31.3 8.5 %shard_map.131 = (bf16[384,512]{1,0:T(8,128)(2,1)}, bf16[6,768,512]{2,1,0:T(8,128)(2,1)}, f32[6,8,512]{2,1,0:T(8,128)}, bf16[384,512]{1,0:T(8,128)(2,1)}, bf16[5...) custom-call(s32[1]{0:T(128)} %bitcast.lat_ref.refs_0_, ...), custom_call_target="tpu_custom_call" | custom-call | flops 6400000000 | bytes 8000000 | tf_op jit(solution)/shard_map/pallas_call | solution.py:548
  39.8 1.9 collective-permute-done.7.n3.refs_5_
  42.2 1.8 collective-permute-start.11
  44.0 2.9 %collective-permute-start.12 = (bf16[32,384]{1,0:T(8,128)(2,1)}, bf16[32,384]{1,0:T(8,128)(2,1)S(1)}, u32[]{:S(2)}, u32[]{:S(2)}) collective-permute-start(bf16[32,384]{1,0:T(8,128)(2,1)} %get-tuple-element.121), channel_id=1, source_target_pairs={{0,14},{2,0},{4,2},{6,4},{8,6},{10,8},{12,10},{14,12},{1,15},{3,1}... | collective-permute-start | bytes 73736 | tf_op jit(solution)/shard_map/ppermute | solution.py:48
  47.8 8.7 %shard_map.132 = (bf16[384,512]{1,0:T(8,128)(2,1)}, bf16[6,768,512]{2,1,0:T(8,128)(2,1)}, f32[6,8,512]{2,1,0:T(8,128)}, bf16[384,512]{1,0:T(8,128)(2,1)}, bf16[5...) custom-call(s32[1]{0:T(128)} %bitcast.lat_ref.refs_0_, ...), custom_call_target="tpu_custom_call" | custom-call | flops 6400000000 | bytes 8000000 | tf_op jit(solution)/shard_map/pallas_call | solution.py:548
  58.6 22.0 %shard_map.133 = (bf16[1024,768]{1,0:T(8,128)(2,1)}, bf16[1536,384]{1,0:T(8,128)(2,1)}, bf16[32,384]{1,0:T(8,128)(2,1)}, bf16[48,384]{1,0:T(8,128)(2,1)}, bf16[48,384]{1,0:T(8,128)(2,1)}) custom-call(s32[1]{0:T(128)} %bitcast.lat_ref.refs_0_, s32[1024,1]{1,0:T(8,128)} %constant.92.clone.place_ref, bf16[512,384]{1,0:T(8,128)(2,1)} %get-tuple-element.106.na_ref, ...), custom_call_target="tpu_custom_call" | custom-call | flops 17600000000 | bytes 22000000 | tf_op jit(solution)/shard_map/pallas_call | solution.py:588
  82.2 4.7 %collective-permute-start.17 = (bf16[48,384]{1,0:T(8,128)(2,1)S(1)}, bf16[48,384]{1,0:T(8,128)(2,1)S(1)}, u32[]{:S(2)}, u32[]{:S(2)}) collective-permute-start(bf16[48,384]{1,0:T(8,128)(2,1)S(1)} %copy-done.26), channel_id=1, source_target_pairs={{0,14},{2,0},{4,2},{6,4},{8,6},{10,8},{12,10},{14,12},{1,15},{3,1}... | collective-permute-start | bytes 110600 | tf_op jit(solution)/shard_map/ppermute | solution.py:48
  87.3 14.9 %shard_map.134 = (f32[512,384]{1,0:T(8,128)}, bf16[512,384]{1,0:T(8,128)(2,1)}, bf16[512,384]{1,0:T(8,128)(2,1)}, bf16[512,384]{1,0:T(8,128)(2,1)}, bf16[512,384...) custom-call(s32[1]{0:T(128)} %bitcast.lat_ref.refs_0_, ...), custom_call_target="tpu_custom_call" | custom-call | flops 10400000000 | bytes 13000000 | tf_op jit(solution)/shard_map/pallas_call | solution.py:635
  106.1 15.8 %shard_map.135 = (f32[512,384]{1,0:T(8,128)}, bf16[512,384]{1,0:T(8,128)(2,1)}, bf16[512,384]{1,0:T(8,128)(2,1)}, bf16[512,384]{1,0:T(8,128)(2,1)}, bf16[512,384...) custom-call(s32[1]{0:T(128)} %bitcast.lat_ref.refs_0_, ...), custom_call_target="tpu_custom_call" | custom-call | flops 10400000000 | bytes 13000000 | tf_op jit(solution)/shard_map/pallas_call | solution.py:635
  125.8 3.0 %collective-permute-start.33 = (bf16[96,384]{1,0:T(8,128)(2,1)S(1)}, bf16[96,384]{1,0:T(8,128)(2,1)}, u32[]{:S(2)}, u32[]{:S(2)}) collective-permute-start(bf16[96,384]{1,0:T(8,128)(2,1)S(1)} %get-tuple-element.202), channel_id=1, source_target_pairs={{0,12},{2,14},{4,8},{6,10},{8,4},{10,6},{12,0},{14,2},{1,13},{3,15... | collective-permute-start | bytes 221192 | tf_op jit(solution)/shard_map/ppermute | solution.py:85
  129.9 1.9 %collective-permute-start.30 = (bf16[384,384]{1,0:T(8,128)(2,1)S(1)}, bf16[384,384]{1,0:T(8,128)(2,1)S(1)}, u32[]{:S(2)}, u32[]{:S(2)}) collective-permute-start(bf16[384,384]{1,0:T(8,128)(2,1)S(1)} %constant_dynamic-slice_fusion.6), channel_id=1, source_target_pairs={{0,2},{2,0},{4,6},{6,4},{8,10},{10,8},{12,14},{14,12},{1,3},{3,1},... | collective-permute-start | bytes 884744 | tf_op jit(solution)/shard_map/ppermute | solution.py:85
  132.0 3.1 %collective-permute-start.34 = (bf16[512,384]{1,0:T(8,128)(2,1)S(1)}, bf16[512,384]{1,0:T(8,128)(2,1)S(1)}, u32[]{:S(2)}, u32[]{:S(2)}) collective-permute-start(bf16[512,384]{1,0:T(8,128)(2,1)S(1)} %add_convert_fusion.3), channel_id=1, source_target_pairs={{0,12},{2,6},{4,0},{6,10},{8,4},{10,14},{12,8},{14,2},{1,13},{3,7}... | collective-permute-start | bytes 1179656 | tf_op jit(solution)/shard_map/ppermute | solution.py:48
  136.1 3.8 %collective-permute-done.30 = bf16[384,384]{1,0:T(8,128)(2,1)S(1)} collective-permute-done((bf16[384,384]{1,0:T(8,128)(2,1)S(1)}, bf16[384,384]{1,0:T(8,128)(2,1)S(1)}, u32[]{:S(2)}, u32[]{:S(2)}) %collective-permute-start.30) | collective-permute-done | bytes 294944 | tf_op jit(solution)/shard_map/ppermute | solution.py:85
  139.9 2.6 %collective-permute-done.34 = bf16[512,384]{1,0:T(8,128)(2,1)S(1)} collective-permute-done((bf16[512,384]{1,0:T(8,128)(2,1)S(1)}, bf16[512,384]{1,0:T(8,128)(2,1)S(1)}, u32[]{:S(2)}, u32[]{:S(2)}) %collective-permute-start.34) | collective-permute-done | bytes 393248 | tf_op jit(solution)/shard_map/ppermute | solution.py:48
  142.7 4.6 %collective-permute-done.35.refs_8_ = bf16[512,384]{1,0:T(8,128)(2,1)S(1)} collective-permute-done((bf16[512,384]{1,0:T(8,128)(2,1)S(1)}, bf16[512,384]{1,0:T(8,128)(2,1)S(1)}, u32[]{:S(2)}, u32[]{:S(2)}) %collective-permute-start.35) | collective-permute-done | bytes 393248 | tf_op jit(solution)/shard_map/ppermute | solution.py:48
  149.7 2.5 %collective-permute-start.37 = (bf16[96,384]{1,0:T(8,128)(2,1)S(1)}, bf16[96,384]{1,0:T(8,128)(2,1)S(1)}, u32[]{:S(2)}, u32[]{:S(2)}) collective-permute-start(bf16[96,384]{1,0:T(8,128)(2,1)S(1)} %get-tuple-element.200), channel_id=1, source_target_pairs={{0,8},{2,10},{4,12},{6,14},{8,0},{10,2},{12,4},{14,6},{1,9},{3,11}... | collective-permute-start | bytes 221192 | tf_op jit(solution)/shard_map/ppermute | solution.py:85
  153.5 2.9 %collective-permute-done.37 = bf16[96,384]{1,0:T(8,128)(2,1)S(1)} collective-permute-done((bf16[96,384]{1,0:T(8,128)(2,1)S(1)}, bf16[96,384]{1,0:T(8,128)(2,1)S(1)}, u32[]{:S(2)}, u32[]{:S(2)}) %collective-permute-start.37) | collective-permute-done | bytes 73760 | tf_op jit(solution)/shard_map/ppermute | solution.py:85
  156.5 1.9 %collective-permute-done.38 = bf16[96,384]{1,0:T(8,128)(2,1)S(1)} collective-permute-done((bf16[96,384]{1,0:T(8,128)(2,1)S(1)}, bf16[96,384]{1,0:T(8,128)(2,1)S(1)}, u32[]{:S(2)}, u32[]{:S(2)}) %collective-permute-start.38) | collective-permute-done | bytes 73760 | tf_op jit(solution)/shard_map/ppermute | solution.py:85
  158.6 1.9 %collective-permute-start.41 = (bf16[192,384]{1,0:T(8,128)(2,1)S(1)}, bf16[192,384]{1,0:T(8,128)(2,1)S(1)}, u32[]{:S(2)}, u32[]{:S(2)}) collective-permute-start(bf16[192,384]{1,0:T(8,128)(2,1)S(1)} %constant_dynamic-update-slice_fusion.5), channel_id=1, source_target_pairs={{0,8},{2,10},{4,12},{6,14},{8,0},{10,2},{12,4},{14,6},{1,9},{3,11}... | collective-permute-start | bytes 442376 | tf_op jit(solution)/shard_map/ppermute | solution.py:105
  160.5 2.4 %collective-permute-start.42 = (bf16[192,384]{1,0:T(8,128)(2,1)S(1)}, bf16[192,384]{1,0:T(8,128)(2,1)S(1)}, u32[]{:S(2)}, u32[]{:S(2)}) collective-permute-start(bf16[192,384]{1,0:T(8,128)(2,1)S(1)} %constant_dynamic-update-slice_fusion.5), channel_id=1, source_target_pairs={{0,12},{2,14},{4,8},{6,10},{8,4},{10,6},{12,0},{14,2},{1,13},{3,15... | collective-permute-start | bytes 442376 | tf_op jit(solution)/shard_map/ppermute | solution.py:105
  163.0 3.1 %collective-permute-done.40 = bf16[192,384]{1,0:T(8,128)(2,1)S(1)} collective-permute-done((bf16[192,384]{1,0:T(8,128)(2,1)S(1)}, bf16[192,384]{1,0:T(8,128)(2,1)S(1)}, u32[]{:S(2)}, u32[]{:S(2)}) %collective-permute-start.40) | collective-permute-done | bytes 147488 | tf_op jit(solution)/shard_map/ppermute | solution.py:105
  166.2 4.5 %collective-permute-done.41 = bf16[192,384]{1,0:T(8,128)(2,1)S(1)} collective-permute-done((bf16[192,384]{1,0:T(8,128)(2,1)S(1)}, bf16[192,384]{1,0:T(8,128)(2,1)S(1)}, u32[]{:S(2)}, u32[]{:S(2)}) %collective-permute-start.41) | collective-permute-done | bytes 147488 | tf_op jit(solution)/shard_map/ppermute | solution.py:105
  172.0 7.8 %shard_map.136 = f32[1024,384]{1,0:T(8,128)} custom-call(s32[1024,1]{1,0:T(8,128)} %constant.92.clone.place_ref, s32[32,32]{1,0:T(8,128)} %vis_ref.5, f32[2,384]{1,0:T(2,128)} %gain_ref.13, f32[1024,384]{1,0:T(8,128)} %bitcast.11, bf16[512,384]{1,0:T(8,128)(2,1)} %get-tuple-element.104.start_ref.refs_0_, f32[512,384]{1,0:T(8,128)} %get-tuple-element.185.refs_1_, ...), custom_call_target="tpu_custom_call" | custom-call | flops 4800000000 | bytes 6000000 | tf_op jit(solution)/shard_map/pallas_call | solution.py:811
  180.8 2.8 %collective-permute-done.44.other_ref = bf16[1536,384]{1,0:T(8,128)(2,1)S(1)} collective-permute-done((bf16[1536,384]{1,0:T(8,128)(2,1)S(1)}, bf16[1536,384]{1,0:T(8,128)(2,1)S(1)}, u32[]{:S(2)}, u32[]{:S(2)}) %collective-permute-start.44) | collective-permute-done | bytes 1179680 | tf_op jit(solution)/shard_map/ppermute | solution.py:48
  183.7 3.6 %shard_map.137 = (f32[2,384,1152]{2,1,0:T(8,128)}, f32[2,384,384]{2,1,0:T(8,128)}, f32[2,384]{1,0:T(2,128)}) custom-call(s32[1]{0:T(128)} %bitcast.lat_ref.refs_0_, bf16[1536,384]{1,0:T(8,128)(2,1)S(1)} %constant_dynamic-update-slice_fusion.7.mine_ref, bf16[1536,384]{1,0:T(8,128)(2,1)S(1)} %collective-permute-done.44.other_ref, ...), custom_call_target="tpu_custom_call" | custom-call | flops 4000000000 | bytes 5000000 | tf_op jit(solution)/shard_map/pallas_call | solution.py:823
  (164 shorter events, 26.9 us)
Async XLA Ops:
  3.9 12.3 %collective-permute-start.1 = (bf16[512,384]{1,0:T(8,128)(2,1)}, bf16[512,384]{1,0:T(8,128)(2,1)S(1)}, u32[]{:S(2)}, u32[]{:S(2)}) collective-permute-start(bf16[512,384]{1,0:T(8,128)(2,1)} %get-tuple-element.101.n0), channel_id=1, source_target_pairs={{0,2},{2,0},{4,6},{6,4},{8,10},{10,8},{12,14},{14,12},{1,3},{3,1},... | collective-permute-start | bytes 1179656 | tf_op jit(solution)/shard_map/ppermute | solution.py:48
  16.1 12.1 %collective-permute-start.2 = (bf16[512,384]{1,0:T(8,128)(2,1)S(1)}, bf16[512,384]{1,0:T(8,128)(2,1)S(1)}, u32[]{:S(2)}, u32[]{:S(2)}) collective-permute-start(bf16[512,384]{1,0:T(8,128)(2,1)S(1)} %collective-permute-done.1.n2), channel_id=1, source_target_pairs={{0,4},{2,14},{4,8},{6,2},{8,12},{10,6},{12,0},{14,10},{1,5},{3,15}... | collective-permute-start | bytes 1179656 | tf_op jit(solution)/shard_map/ppermute | solution.py:48
  17.9 11.7 %collective-permute-start.6 = (bf16[512,384]{1,0:T(8,128)(2,1)}, bf16[512,384]{1,0:T(8,128)(2,1)S(1)}, u32[]{:S(2)}, u32[]{:S(2)}) collective-permute-start(bf16[512,384]{1,0:T(8,128)(2,1)} %get-tuple-element.107.n0.refs_2_), channel_id=1, source_target_pairs={{0,2},{2,0},{4,6},{6,4},{8,10},{10,8},{12,14},{14,12},{1,3},{3,1},... | collective-permute-start | bytes 1179656 | tf_op jit(solution)/shard_map/ppermute | solution.py:48
  21.5 8.2 %collective-permute-start = (bf16[512,384]{1,0:T(8,128)(2,1)S(1)}, bf16[512,384]{1,0:T(8,128)(2,1)S(1)}, u32[]{:S(2)}, u32[]{:S(2)}) collective-permute-start(bf16[512,384]{1,0:T(8,128)(2,1)S(1)} %copy-done.11), channel_id=1, source_target_pairs={{0,1},{1,0},{2,3},{3,2},{4,5},{5,4},{6,7},{7,6},{8,9},{9,8},{10,11... | collective-permute-start | bytes 1179656 | tf_op jit(solution)/shard_map/ppermute | solution.py:48
  21.5 8.3 %collective-permute-start.3 = (bf16[512,384]{1,0:T(8,128)(2,1)S(1)}, bf16[512,384]{1,0:T(8,128)(2,1)S(1)}, u32[]{:S(2)}, u32[]{:S(2)}) collective-permute-start(bf16[512,384]{1,0:T(8,128)(2,1)S(1)} %collective-permute-done.1.n2), channel_id=1, source_target_pairs={{0,1},{1,0},{2,3},{3,2},{4,5},{5,4},{6,7},{7,6},{8,9},{9,8},{10,11... | collective-permute-start | bytes 1179656 | tf_op jit(solution)/shard_map/ppermute | solution.py:48
  28.2 15.7 %collective-permute-start.5 = (bf16[512,384]{1,0:T(8,128)(2,1)}, bf16[512,384]{1,0:T(8,128)(2,1)S(1)}, u32[]{:S(2)}, u32[]{:S(2)}) collective-permute-start(bf16[512,384]{1,0:T(8,128)(2,1)} %get-tuple-element.107.n0.refs_2_), channel_id=1, source_target_pairs={{0,1},{1,0},{2,3},{3,2},{4,5},{5,4},{6,7},{7,6},{8,9},{9,8},{10,11... | collective-permute-start | bytes 1179656 | tf_op jit(solution)/shard_map/ppermute | solution.py:48
  29.7 12.0 %collective-permute-start.7 = (bf16[512,384]{1,0:T(8,128)(2,1)S(1)}, bf16[512,384]{1,0:T(8,128)(2,1)S(1)}, u32[]{:S(2)}, u32[]{:S(2)}) collective-permute-start(bf16[512,384]{1,0:T(8,128)(2,1)S(1)} %collective-permute-done.6.n2.refs_4_), channel_id=1, source_target_pairs={{0,4},{2,14},{4,8},{6,2},{8,12},{10,6},{12,0},{14,10},{1,5},{3,15}... | collective-permute-start | bytes 1179656 | tf_op jit(solution)/shard_map/ppermute | solution.py:48
  29.7 17.2 %collective-permute-start.8 = (bf16[512,384]{1,0:T(8,128)(2,1)S(1)}, bf16[512,384]{1,0:T(8,128)(2,1)S(1)}, u32[]{:S(2)}, u32[]{:S(2)}) collective-permute-start(bf16[512,384]{1,0:T(8,128)(2,1)S(1)} %collective-permute-done.6.n2.refs_4_), channel_id=1, source_target_pairs={{0,1},{1,0},{2,3},{3,2},{4,5},{5,4},{6,7},{7,6},{8,9},{9,8},{10,11... | collective-permute-start | bytes 1179656 | tf_op jit(solution)/shard_map/ppermute | solution.py:48
  41.6 5.2 %collective-permute-start.9 = (bf16[512,384]{1,0:T(8,128)(2,1)S(1)}, bf16[512,384]{1,0:T(8,128)(2,1)S(1)}, u32[]{:S(2)}, u32[]{:S(2)}) collective-permute-start(bf16[512,384]{1,0:T(8,128)(2,1)S(1)} %collective-permute-done.7.n3.refs_5_), channel_id=1, source_target_pairs={{0,1},{1,0},{2,3},{3,2},{4,5},{5,4},{6,7},{7,6},{8,9},{9,8},{10,11... | collective-permute-start | bytes 1179656 | tf_op jit(solution)/shard_map/ppermute | solution.py:48
  41.6 14.8 %collective-permute-start.10 = (bf16[32,384]{1,0:T(8,128)(2,1)}, bf16[32,384]{1,0:T(8,128)(2,1)S(1)}, u32[]{:S(2)}, u32[]{:S(2)}) collective-permute-start(bf16[32,384]{1,0:T(8,128)(2,1)} %get-tuple-element.119), channel_id=1, source_target_pairs={{0,1},{1,0},{2,3},{3,2},{4,5},{5,4},{6,7},{7,6},{8,9},{9,8},{10,11... | collective-permute-start | bytes 73736 | tf_op jit(solution)/shard_map/ppermute | solution.py:48
  42.2 14.3 %collective-permute-start.11 = (bf16[32,384]{1,0:T(8,128)(2,1)}, bf16[32,384]{1,0:T(8,128)(2,1)S(1)}, u32[]{:S(2)}, u32[]{:S(2)}) collective-permute-start(bf16[32,384]{1,0:T(8,128)(2,1)} %get-tuple-element.120), channel_id=1, source_target_pairs={{0,2},{2,4},{4,6},{6,8},{8,10},{10,12},{12,14},{14,0},{1,3},{3,5},... | collective-permute-start | bytes 73736 | tf_op jit(solution)/shard_map/ppermute | solution.py:48
  44.0 12.5 %collective-permute-start.12 = (bf16[32,384]{1,0:T(8,128)(2,1)}, bf16[32,384]{1,0:T(8,128)(2,1)S(1)}, u32[]{:S(2)}, u32[]{:S(2)}) collective-permute-start(bf16[32,384]{1,0:T(8,128)(2,1)} %get-tuple-element.121), channel_id=1, source_target_pairs={{0,14},{2,0},{4,2},{6,4},{8,6},{10,8},{12,10},{14,12},{1,15},{3,1}... | collective-permute-start | bytes 73736 | tf_op jit(solution)/shard_map/ppermute | solution.py:48
  82.2 20.1 %collective-permute-start.16 = (bf16[48,384]{1,0:T(8,128)(2,1)}, bf16[48,384]{1,0:T(8,128)(2,1)S(1)}, u32[]{:S(2)}, u32[]{:S(2)}) collective-permute-start(bf16[48,384]{1,0:T(8,128)(2,1)} %get-tuple-element.127), channel_id=1, source_target_pairs={{0,2},{2,4},{4,6},{6,8},{8,10},{10,12},{12,14},{14,0},{1,3},{3,5},... | collective-permute-start | bytes 110600 | tf_op jit(solution)/shard_map/ppermute | solution.py:48
  82.2 20.1 %collective-permute-start.17 = (bf16[48,384]{1,0:T(8,128)(2,1)S(1)}, bf16[48,384]{1,0:T(8,128)(2,1)S(1)}, u32[]{:S(2)}, u32[]{:S(2)}) collective-permute-start(bf16[48,384]{1,0:T(8,128)(2,1)S(1)} %copy-done.26), channel_id=1, source_target_pairs={{0,14},{2,0},{4,2},{6,4},{8,6},{10,8},{12,10},{14,12},{1,15},{3,1}... | collective-permute-start | bytes 110600 | tf_op jit(solution)/shard_map/ppermute | solution.py:48
  87.0 15.3 %collective-permute-start.15 = (bf16[32,384]{1,0:T(8,128)(2,1)}, bf16[32,384]{1,0:T(8,128)(2,1)S(1)}, u32[]{:S(2)}, u32[]{:S(2)}) collective-permute-start(bf16[32,384]{1,0:T(8,128)(2,1)} %get-tuple-element.126), channel_id=1, source_target_pairs={{0,1},{1,0},{2,3},{3,2},{4,5},{5,4},{6,7},{7,6},{8,9},{9,8},{10,11... | collective-permute-start | bytes 73736 | tf_op jit(solution)/shard_map/ppermute | solution.py:48
  87.2 15.0 %collective-permute-start.19 = (bf16[384,384]{1,0:T(8,128)(2,1)S(1)}, bf16[384,384]{1,0:T(8,128)(2,1)S(1)}, u32[]{:S(2)}, u32[]{:S(2)}) collective-permute-start(bf16[384,384]{1,0:T(8,128)(2,1)S(1)} %constant_dynamic-slice_fusion.7), channel_id=1, source_target_pairs={{0,2},{2,0},{4,6},{6,4},{8,10},{10,8},{12,14},{14,12},{1,3},{3,1},... | collective-permute-start | bytes 884744 | tf_op jit(solution)/shard_map/ppermute | solution.py:85
  105.7 16.3 %collective-permute-start.25 = (bf16[512,384]{1,0:T(8,128)(2,1)S(1)}, bf16[512,384]{1,0:T(8,128)(2,1)S(1)}, u32[]{:S(2)}, u32[]{:S(2)}) collective-permute-start(bf16[512,384]{1,0:T(8,128)(2,1)S(1)} %add_convert_fusion.6), channel_id=1, source_target_pairs={{0,12},{2,6},{4,0},{6,10},{8,4},{10,14},{12,8},{14,2},{1,13},{3,7}... | collective-permute-start | bytes 1179656 | tf_op jit(solution)/shard_map/ppermute | solution.py:48
  123.4 5.5 %collective-permute-start.26 = (bf16[768,384]{1,0:T(8,128)(2,1)}, bf16[768,384]{1,0:T(8,128)(2,1)S(1)}, u32[]{:S(2)}, u32[]{:S(2)}) collective-permute-start(bf16[768,384]{1,0:T(8,128)(2,1)} %get-tuple-element.170), channel_id=1, source_target_pairs={{0,1},{1,0},{2,3},{3,2},{4,5},{5,4},{6,7},{7,6},{8,9},{9,8},{10,11... | collective-permute-start | bytes 1769480 | tf_op jit(solution)/shard_map/ppermute | solution.py:48
  123.5 5.6 %collective-permute-start.27 = (bf16[512,384]{1,0:T(8,128)(2,1)}, bf16[512,384]{1,0:T(8,128)(2,1)S(1)}, u32[]{:S(2)}, u32[]{:S(2)}) collective-permute-start(bf16[512,384]{1,0:T(8,128)(2,1)} %get-tuple-element.171), channel_id=1, source_target_pairs={{0,1},{1,0},{2,3},{3,2},{4,5},{5,4},{6,7},{7,6},{8,9},{9,8},{10,11... | collective-permute-start | bytes 1179656 | tf_op jit(solution)/shard_map/ppermute | solution.py:48
  124.0 8.0 %collective-permute-start.31 = (bf16[96,384]{1,0:T(8,128)(2,1)S(1)}, bf16[96,384]{1,0:T(8,128)(2,1)S(1)}, u32[]{:S(2)}, u32[]{:S(2)}) collective-permute-start(bf16[96,384]{1,0:T(8,128)(2,1)S(1)} %get-tuple-element.201), channel_id=1, source_target_pairs={{0,4},{2,6},{4,0},{6,2},{8,12},{10,14},{12,8},{14,10},{1,5},{3,7},... | collective-permute-start | bytes 221192 | tf_op jit(solution)/shard_map/ppermute | solution.py:85
  125.7 9.4 %collective-permute-start.32 = (bf16[96,384]{1,0:T(8,128)(2,1)S(1)}, bf16[96,384]{1,0:T(8,128)(2,1)S(1)}, u32[]{:S(2)}, u32[]{:S(2)}) collective-permute-start(bf16[96,384]{1,0:T(8,128)(2,1)S(1)} %get-tuple-element.203), channel_id=1, source_target_pairs={{0,8},{2,10},{4,12},{6,14},{8,0},{10,2},{12,4},{14,6},{1,9},{3,11}... | collective-permute-start | bytes 221192 | tf_op jit(solution)/shard_map/ppermute | solution.py:85
  125.8 9.3 %collective-permute-start.33 = (bf16[96,384]{1,0:T(8,128)(2,1)S(1)}, bf16[96,384]{1,0:T(8,128)(2,1)}, u32[]{:S(2)}, u32[]{:S(2)}) collective-permute-start(bf16[96,384]{1,0:T(8,128)(2,1)S(1)} %get-tuple-element.202), channel_id=1, source_target_pairs={{0,12},{2,14},{4,8},{6,10},{8,4},{10,6},{12,0},{14,2},{1,13},{3,15... | collective-permute-start | bytes 221192 | tf_op jit(solution)/shard_map/ppermute | solution.py:85
  129.9 9.9 %collective-permute-start.30 = (bf16[384,384]{1,0:T(8,128)(2,1)S(1)}, bf16[384,384]{1,0:T(8,128)(2,1)S(1)}, u32[]{:S(2)}, u32[]{:S(2)}) collective-permute-start(bf16[384,384]{1,0:T(8,128)(2,1)S(1)} %constant_dynamic-slice_fusion.6), channel_id=1, source_target_pairs={{0,2},{2,0},{4,6},{6,4},{8,10},{10,8},{12,14},{14,12},{1,3},{3,1},... | collective-permute-start | bytes 884744 | tf_op jit(solution)/shard_map/ppermute | solution.py:85
  131.8 15.5 %collective-permute-start.35 = (bf16[512,384]{1,0:T(8,128)(2,1)S(1)}, bf16[512,384]{1,0:T(8,128)(2,1)S(1)}, u32[]{:S(2)}, u32[]{:S(2)}) collective-permute-start(bf16[512,384]{1,0:T(8,128)(2,1)S(1)} %add_convert_fusion.5), channel_id=1, source_target_pairs={{0,2},{2,0},{4,6},{6,4},{8,10},{10,8},{12,14},{14,12},{1,3},{3,1},... | collective-permute-start | bytes 1179656 | tf_op jit(solution)/shard_map/ppermute | solution.py:48
  132.0 10.6 %collective-permute-start.34 = (bf16[512,384]{1,0:T(8,128)(2,1)S(1)}, bf16[512,384]{1,0:T(8,128)(2,1)S(1)}, u32[]{:S(2)}, u32[]{:S(2)}) collective-permute-start(bf16[512,384]{1,0:T(8,128)(2,1)S(1)} %add_convert_fusion.3), channel_id=1, source_target_pairs={{0,12},{2,6},{4,0},{6,10},{8,4},{10,14},{12,8},{14,2},{1,13},{3,7}... | collective-permute-start | bytes 1179656 | tf_op jit(solution)/shard_map/ppermute | solution.py:48
  147.3 11.1 %collective-permute-start.39 = (bf16[512,384]{1,0:T(8,128)(2,1)S(1)}, bf16[512,384]{1,0:T(8,128)(2,1)S(1)}, u32[]{:S(2)}, u32[]{:S(2)}) collective-permute-start(bf16[512,384]{1,0:T(8,128)(2,1)S(1)} %add_convert_fusion.2), channel_id=1, source_target_pairs={{0,2},{2,0},{4,6},{6,4},{8,10},{10,8},{12,14},{14,12},{1,3},{3,1},... | collective-permute-start | bytes 1179656 | tf_op jit(solution)/shard_map/ppermute | solution.py:48
  149.7 6.8 %collective-permute-start.37 = (bf16[96,384]{1,0:T(8,128)(2,1)S(1)}, bf16[96,384]{1,0:T(8,128)(2,1)S(1)}, u32[]{:S(2)}, u32[]{:S(2)}) collective-permute-start(bf16[96,384]{1,0:T(8,128)(2,1)S(1)} %get-tuple-element.200), channel_id=1, source_target_pairs={{0,8},{2,10},{4,12},{6,14},{8,0},{10,2},{12,4},{14,6},{1,9},{3,11}... | collective-permute-start | bytes 221192 | tf_op jit(solution)/shard_map/ppermute | solution.py:85
  152.2 6.2 %collective-permute-start.38 = (bf16[96,384]{1,0:T(8,128)(2,1)S(1)}, bf16[96,384]{1,0:T(8,128)(2,1)S(1)}, u32[]{:S(2)}, u32[]{:S(2)}) collective-permute-start(bf16[96,384]{1,0:T(8,128)(2,1)S(1)} %get-tuple-element.199), channel_id=1, source_target_pairs={{0,12},{2,14},{4,8},{6,10},{8,4},{10,6},{12,0},{14,2},{1,13},{3,15... | collective-permute-start | bytes 221192 | tf_op jit(solution)/shard_map/ppermute | solution.py:85
  158.5 7.7 %collective-permute-start.40 = (bf16[192,384]{1,0:T(8,128)(2,1)S(1)}, bf16[192,384]{1,0:T(8,128)(2,1)S(1)}, u32[]{:S(2)}, u32[]{:S(2)}) collective-permute-start(bf16[192,384]{1,0:T(8,128)(2,1)S(1)} %constant_dynamic-update-slice_fusion.5), channel_id=1, source_target_pairs={{0,4},{2,6},{4,0},{6,2},{8,12},{10,14},{12,8},{14,10},{1,5},{3,7},... | collective-permute-start | bytes 442376 | tf_op jit(solution)/shard_map/ppermute | solution.py:105
  158.6 12.1 %collective-permute-start.41 = (bf16[192,384]{1,0:T(8,128)(2,1)S(1)}, bf16[192,384]{1,0:T(8,128)(2,1)S(1)}, u32[]{:S(2)}, u32[]{:S(2)}) collective-permute-start(bf16[192,384]{1,0:T(8,128)(2,1)S(1)} %constant_dynamic-update-slice_fusion.5), channel_id=1, source_target_pairs={{0,8},{2,10},{4,12},{6,14},{8,0},{10,2},{12,4},{14,6},{1,9},{3,11}... | collective-permute-start | bytes 442376 | tf_op jit(solution)/shard_map/ppermute | solution.py:105
  160.5 10.2 %collective-permute-start.42 = (bf16[192,384]{1,0:T(8,128)(2,1)S(1)}, bf16[192,384]{1,0:T(8,128)(2,1)S(1)}, u32[]{:S(2)}, u32[]{:S(2)}) collective-permute-start(bf16[192,384]{1,0:T(8,128)(2,1)S(1)} %constant_dynamic-update-slice_fusion.5), channel_id=1, source_target_pairs={{0,12},{2,14},{4,8},{6,10},{8,4},{10,6},{12,0},{14,2},{1,13},{3,15... | collective-permute-start | bytes 442376 | tf_op jit(solution)/shard_map/ppermute | solution.py:105
  170.7 9.9 %collective-permute-start.43 = (bf16[768,384]{1,0:T(8,128)(2,1)S(1)}, bf16[768,384]{1,0:T(8,128)(2,1)S(1)}, u32[]{:S(2)}, u32[]{:S(2)}) collective-permute-start(bf16[768,384]{1,0:T(8,128)(2,1)S(1)} %constant_dynamic-update-slice_fusion.9), channel_id=1, source_target_pairs={{0,2},{2,0},{4,6},{6,4},{8,10},{10,8},{12,14},{14,12},{1,3},{3,1},... | collective-permute-start | bytes 1769480 | tf_op jit(solution)/shard_map/ppermute | solution.py:105
  (45 other events, 176.0 us)
